TPU v7x, 1024 devices: a whole 4x4x32 slice. The times are simulated.
1024 devices in a mesh: seq: 64 (over y, z_hi, x), head: 16 (over z_lo, core).
Axes of the slice: x: 4, y: 4, z: 32 (z_hi: 4, z_lo: 8; z = z_hi * 8 + z_lo), core: 2. Of those that a mesh axis runs over, the one named last changes fastest.
Arguments:
- queries: bfloat16 [32768, 64, 128], P('seq', 'head'), may hold values from -48 to 48
- keys_values: bfloat16 [32768, 2, 8, 128], P('seq'), may hold values from -6 to 6
- grad_out: bfloat16 [32768, 64, 128], P('seq', 'head'), may hold values from -6 to 6
- segments: int32 [32768], P('seq'), may hold values from 0 to 14, as said below
- partner: int32 [64], replicated, may hold values from 0 to 63, as said below
- prompt_blocks: int32 [64], replicated, may hold values from 1 to 4, as said below
Outputs:
- attention: bfloat16 [32768, 64, 128], P('seq', 'head')
- query_gradient: bfloat16 [32768, 64, 128], P('seq', 'head')
- kv_grad: bfloat16 [32768, 2048], P('seq', 'head')
Inputs may be any that keep to these rules, and one draw needn't show every extreme that they name: `segments`: within each bin ids never fall; segment 0 begins at the bin's first token and holds more than 64 tokens; segment 1 follows it directly and is the bin's rejected response; the largest id is reached in some bin in every draw. partner[b] != b, every bin is the partner of exactly one bin, and following partner from any bin visits all bins. `prompt_blocks`: the largest value is reached in every draw.
All inputs are finite; a program needn't handle non-finite values.
Results may differ from a plain program's by a relative error of at most 0.025.
Values may be sent and summed in bfloat16 or wider, within the bound.
No kernel may reach another device: no remote copies, remote signals or barrier semaphores. Data moves between devices by JAX's collectives and lax.ppermute only.
A program may use at most 32 MiB of HBM per device.

v0:
```python
import math

import jax
import jax.numpy as jnp
from jax import lax
from jax.sharding import PartitionSpec as P

HEADS = 64
KVH = 8
PMAX = 64
BLK = 16


def from_partner(value, axis, apart):
    mask = 2**apart
    pairs = [(source, source ^ mask) for source in range(lax.axis_size(axis))]
    return lax.ppermute(value, axis, pairs)


def slotted(parcel, wanted):
    mask = wanted.reshape((-1,) + (1,) * parcel.ndim)
    return jnp.where(mask, parcel[None], jnp.zeros((), parcel.dtype))


def head_total(block, sharing):
    flat = block.reshape(block.shape[0], -1)
    place = lax.axis_index("head")
    for bit in reversed(range(sharing.bit_length() - 1)):
        half = flat.shape[1] // 2
        mine = place // 2**bit % 2
        kept = lax.dynamic_slice_in_dim(flat, mine * half, half, 1)
        given = lax.dynamic_slice_in_dim(flat, (1 - mine) * half, half, 1)
        got = from_partner(given.astype(jnp.bfloat16), "head", bit).astype(given.dtype)
        flat = kept + got
    return flat


def body(queries, keys_values, grad_out, segments, partner, prompt_blocks):
    rows_here = queries.shape[0]
    heads_here = queries.shape[1]
    head_dim = queries.shape[2]
    group_size = HEADS // KVH
    kv_here = max(1, heads_here // group_size)
    per_kv = heads_here // kv_here
    sharing = max(1, group_size // heads_here)
    kv_start = lax.axis_index("head") * heads_here // group_size
    self_index = lax.axis_index("seq")
    bin_count = lax.axis_size("seq")
    score_scaling = 1.0 / math.sqrt(head_dim)
    bin_ids = jnp.arange(bin_count, dtype=jnp.int32)
    owner_bin = partner[self_index]
    source = jnp.sum(jnp.where(partner == self_index, bin_ids, 0))
    kv_local = lax.dynamic_slice_in_dim(keys_values, kv_start, kv_here, 2)
    prompt = kv_local[:PMAX]
    received = lax.all_to_all(
        slotted(prompt, partner == self_index), "seq", split_axis=0, concat_axis=0, tiled=True
    )
    remote = lax.dynamic_index_in_dim(received, owner_bin, 0, keepdims=False)
    every_key_row = jnp.concatenate([kv_local[:, 0], remote[:, 0]], axis=0)
    every_value_row = jnp.concatenate([kv_local[:, 1], remote[:, 1]], axis=0)
    query_by_group = queries.reshape(rows_here, kv_here, per_kv, head_dim)
    gradient_by_group = grad_out.reshape(rows_here, kv_here, per_kv, head_dim)
    positions = jnp.arange(rows_here, dtype=jnp.int32)
    local_ok = (segments[:, None] == segments[None, :]) & (positions[None, :] <= positions[:, None])
    live_count = BLK * prompt_blocks[owner_bin]
    remote_ok = (segments[:, None] == 1) & (jnp.arange(PMAX, dtype=jnp.int32)[None, :] < live_count)
    allowed = jnp.concatenate([local_ok, remote_ok], axis=1)[None, None]
    score_matrix = (
        jnp.einsum(
            "imwh,lmh->mwil", query_by_group, every_key_row, preferred_element_type=jnp.float32
        )
        * score_scaling
    )
    score_matrix = jnp.where(allowed, score_matrix, -jnp.inf)
    row_peak = jnp.max(score_matrix, axis=-1, keepdims=True)
    weights_raw = jnp.where(allowed, jnp.exp(score_matrix - row_peak), jnp.float32(0.0))
    probabilities = weights_raw / jnp.sum(weights_raw, axis=-1, keepdims=True)
    probability_lowprec = probabilities.astype(jnp.bfloat16)
    blended_values = jnp.einsum(
        "aqiu,uax->iaqx", probability_lowprec, every_value_row, preferred_element_type=jnp.float32
    )
    attention = blended_values.astype(jnp.bfloat16)
    row_delta = jnp.sum(
        gradient_by_group.astype(jnp.float32) * attention.astype(jnp.float32), axis=-1
    )
    row_delta = jnp.transpose(row_delta, (1, 2, 0))
    probability_gradient = jnp.einsum(
        "imwh,lmh->mwil", gradient_by_group, every_value_row, preferred_element_type=jnp.float32
    )
    score_gradient = (probabilities * (probability_gradient - row_delta[..., None])).astype(
        jnp.bfloat16
    )
    query_gradient = (
        jnp.einsum(
            "aqiu,uax->iaqx", score_gradient, every_key_row, preferred_element_type=jnp.float32
        )
        * score_scaling
    )
    query_gradient = query_gradient.astype(jnp.bfloat16).reshape(rows_here, heads_here, head_dim)
    key_grad = (
        jnp.einsum(
            "emox,oemn->xen", score_gradient, query_by_group, preferred_element_type=jnp.float32
        )
        * score_scaling
    )
    value_grad = jnp.einsum(
        "emox,oemn->xen", probability_lowprec, gradient_by_group, preferred_element_type=jnp.float32
    )
    kv_grads = jnp.stack([key_grad, value_grad], axis=2).astype(jnp.bfloat16)
    local_part = kv_grads[:rows_here]
    remote_part = kv_grads[rows_here:]
    received_grads = lax.all_to_all(
        slotted(remote_part, bin_ids == owner_bin), "seq", split_axis=0, concat_axis=0, tiled=True
    )
    arrived = lax.dynamic_index_in_dim(received_grads, source, 0, keepdims=False)
    joined = lax.optimization_barrier(jnp.concatenate([local_part, arrived], axis=0))
    summed = head_total(joined.astype(jnp.float32), sharing)
    own_sum = summed[:rows_here]
    prompt_low = summed[rows_here:].astype(jnp.bfloat16)
    prompt_rows = own_sum[:PMAX] + prompt_low.astype(jnp.float32)
    kv_result = jnp.concatenate([prompt_rows, own_sum[PMAX:]], axis=0).astype(jnp.bfloat16)
    return (attention.reshape(rows_here, heads_here, head_dim), query_gradient, kv_result)


def solution(mesh):
    in_specs = (
        P("seq", "head", None),
        P("seq", None, None, None),
        P("seq", "head", None),
        P("seq"),
        P(),
        P(),
    )
    out_specs = (P("seq", "head", None), P("seq", "head", None), P("seq", "head"))
    return jax.shard_map(body, mesh=mesh, in_specs=in_specs, out_specs=out_specs, check_vma=False)
```

profile of v0, /device:TPU:97, one launch (start us, length us, event | category | flops | bytes accessed | tf_op | source)
XLA Modules:
  0.0 441.6 jit_solution(9413057814001892264)
XLA Ops:
  0.7 1.1 constant_dynamic-slice_fusion
  1.8 1.3 select_reduce_fusion
  3.1 1.5 broadcast_select_fusion.1
  4.6 31.5 %all-to-all-start = ((bf16[64,64,2,1,128]{4,1,2,3,0:T(8,128)(2,1)}), bf16[64,64,2,1,128]{4,1,2,3,0:T(8,128)(2,1)S(1)}, u32[]{:S(2)}, u32[]{:S(2)}) async-start(bf16[64,64,2,1,128]{4,1,2,3,0:T(8,128)(2,1)} %broadcast_select_fusion.1), calls=%async_computation | async-start | bytes 4194304 | tf_op jit(solution)/shard_map/all_to_all | solution.py:55
  38.0 1.1 copy.20
  42.1 2.1 constant_dynamic-slice_fusion.2
  44.2 163.4 %all-to-all-done = bf16[64,64,2,1,128]{4,1,2,3,0:T(8,128)(2,1)S(1)} async-done(((bf16[64,64,2,1,128]{4,1,2,3,0:T(8,128)(2,1)}), bf16[64,64,2,1,128]{4,1,2,3,0:T(8,128)(2,1)S(1)}, u32[]{:S(2)}, u32[]{:S(2)}) %all-to-all-start) | async-done | bytes 2097184 | tf_op jit(solution)/shard_map/all_to_all | solution.py:55
  207.7 0.9 fusion.2
  208.6 1.2 fusion.4
  209.8 1.5 fusion.24
  211.3 2.5 fusion.28
  213.8 2.8 fusion.5
  216.6 0.8 fusion.27
  217.4 1.5 broadcast_select_fusion
  218.9 12.0 %all-to-all-start.1 = ((bf16[64,64,1,2,128]{4,1,3,2,0:T(8,128)(2,1)}), bf16[64,64,1,2,128]{4,1,3,2,0:T(8,128)(2,1)}, u32[]{:S(2)}, u32[]{:S(2)}) async-start(bf16[64,64,1,2,128]{4,1,3,2,0:T(8,128)(2,1)} %broadcast_select_fusion), calls=%async_computation.1 | async-start | bytes 4194304 | tf_op jit(solution)/shard_map/all_to_all | solution.py:112
  232.6 105.4 %all-to-all-done.1 = bf16[64,64,1,2,128]{4,1,3,2,0:T(8,128)(2,1)} async-done(((bf16[64,64,1,2,128]{4,1,3,2,0:T(8,128)(2,1)}), bf16[64,64,1,2,128]{4,1,3,2,0:T(8,128)(2,1)}, u32[]{:S(2)}, u32[]{:S(2)}) %all-to-all-start.1) | async-done | bytes 2097184 | tf_op jit(solution)/shard_map/all_to_all | solution.py:112
  338.0 0.8 dynamic-slice_bitcast_fusion
  339.2 0.8 copy-done.1
  340.0 95.2 %collective-permute-start = (bf16[576,128]{1,0:T(8,128)(2,1)S(1)}, bf16[576,128]{1,0:T(8,128)(2,1)}, u32[]{:S(2)}, u32[]{:S(2)}) collective-permute-start(bf16[576,128]{1,0:T(8,128)(2,1)S(1)} %dynamic-slice_convert_fusion), channel_id=1, source_target_pairs={{0,1},{1,0},{2,3},{3,2},{4,5},{5,4},{6,7},{7,6},{8,9},{9,8},{10,11... | collective-permute-start | bytes 442376 | tf_op jit(solution)/shard_map/ppermute | solution.py:17
  435.2 1.5 fusion.15
  436.7 1.1 copy.25
  437.8 2.1 copy.24
  439.9 1.1 fusion.42
  441.0 0.7 pad_maximum_fusion.1
  (40 shorter events, 2.7 us)
Async XLA Ops:
  0.6 207.0 %copy-start = (bf16[512,4,128]{2,1,0:T(4,128)(2,1)S(1)}, bf16[512,4,128]{2,1,0:T(4,128)(2,1)}, u32[]{:S(2)}) copy-start(bf16[512,4,128]{2,1,0:T(4,128)(2,1)} %param.6) | copy-start | bytes 1572868
  0.6 35.5 %copy-start.8 = (s32[64]{0:T(128)S(1)}, s32[64]{0:T(128)}, u32[]{:S(2)}) copy-start(s32[64]{0:T(128)} %param.10) | copy-start | bytes 772
  0.7 37.4 %copy-start.2 = (bf16[512,4,128]{2,1,0:T(4,128)(2,1)S(1)}, bf16[512,4,128]{2,1,0:T(4,128)(2,1)}, u32[]{:S(2)}) copy-start(bf16[512,4,128]{2,1,0:T(4,128)(2,1)} %param.8) | copy-start | bytes 1572868
  0.7 39.1 %copy-start.9 = (s32[64]{0:T(128)S(1)}, s32[64]{0:T(128)}, u32[]{:S(2)}) copy-start(s32[64]{0:T(128)} %param.11) | copy-start | bytes 772
  0.7 41.0 %copy-start.7 = (s32[512]{0:T(512)S(1)}, s32[512]{0:T(512)}, u32[]{:S(2)}) copy-start(s32[512]{0:T(512)} %param.9) | copy-start | bytes 6148
  4.6 203.0 %all-to-all-start = ((bf16[64,64,2,1,128]{4,1,2,3,0:T(8,128)(2,1)}), bf16[64,64,2,1,128]{4,1,2,3,0:T(8,128)(2,1)S(1)}, u32[]{:S(2)}, u32[]{:S(2)}) async-start(bf16[64,64,2,1,128]{4,1,2,3,0:T(8,128)(2,1)} %broadcast_select_fusion.1), calls=%async_computation | async-start | bytes 4194304 | tf_op jit(solution)/shard_map/all_to_all | solution.py:55
  44.2 165.6 %copy-start.4 = (bf16[512,1,128]{2,0,1:T(8,128)(2,1)}, bf16[512,1,128]{2,0,1:T(8,128)(2,1)S(1)}, u32[]{:S(2)}) copy-start(bf16[512,1,128]{2,0,1:T(8,128)(2,1)S(1)} %get-tuple-element.21) | copy-start | bytes 393220
  44.2 167.1 %copy-start.5 = (bf16[512,1,128]{2,0,1:T(8,128)(2,1)}, bf16[512,1,128]{2,0,1:T(8,128)(2,1)S(1)}, u32[]{:S(2)}) copy-start(bf16[512,1,128]{2,0,1:T(8,128)(2,1)S(1)} %get-tuple-element.22) | copy-start | bytes 393220
  207.7 2.1 copy-start.6
  207.7 2.1 copy-start.3
  218.9 119.1 %all-to-all-start.1 = ((bf16[64,64,1,2,128]{4,1,3,2,0:T(8,128)(2,1)}), bf16[64,64,1,2,128]{4,1,3,2,0:T(8,128)(2,1)}, u32[]{:S(2)}, u32[]{:S(2)}) async-start(bf16[64,64,1,2,128]{4,1,3,2,0:T(8,128)(2,1)} %broadcast_select_fusion), calls=%async_computation.1 | async-start | bytes 4194304 | tf_op jit(solution)/shard_map/all_to_all | solution.py:112
  339.2 0.8 copy-start.1
  340.0 99.9 %collective-permute-start = (bf16[576,128]{1,0:T(8,128)(2,1)S(1)}, bf16[576,128]{1,0:T(8,128)(2,1)}, u32[]{:S(2)}, u32[]{:S(2)}) collective-permute-start(bf16[576,128]{1,0:T(8,128)(2,1)S(1)} %dynamic-slice_convert_fusion), channel_id=1, source_target_pairs={{0,1},{1,0},{2,3},{3,2},{4,5},{5,4},{6,7},{7,6},{8,9},{9,8},{10,11... | collective-permute-start | bytes 442376 | tf_op jit(solution)/shard_map/ppermute | solution.py:17
where the time goes:
time: 442 us
  waiting for transfers between devices  269 us (61%)
  starting transfers between devices  139 us (31%)
  local copies, waits for them, and re-layouts  10.7 us (2%)
  matrix products  10 us (2%)
  other arithmetic  8.28 us (2%)
  between operations  5.24 us (1%)
    all_to_all x1, waiting for transfers between devices, body(): lax.all_to_all(slotted(prompt, partner == self_index), 'seq', split_axis=...  163 us
    all_to_all x1, waiting for transfers between devices, body(): lax.all_to_all(slotted(remote_part, bin_ids == owner_bin), 'seq', split_a...  105 us
    ppermute x1, starting transfers between devices, from_partner(): return lax.ppermute(value, axis, pairs)  95.2 us
    all_to_all x1, starting transfers between devices, body(): lax.all_to_all(slotted(prompt, partner == self_index), 'seq', split_axis=...  31.5 us
    all_to_all x1, starting transfers between devices, body(): lax.all_to_all(slotted(remote_part, bin_ids == owner_bin), 'seq', split_a...  12 us
  transfers between devices with their start and end apart: 3, of which 2 were waited for; matrix products, arithmetic and copies ran while one was open for 2% of the time, Pallas kernels for 0%

commit v1 on v0

v1 whole, which is shorter than its diff:
```python
import math

import jax
import jax.numpy as jnp
from jax import lax
from jax.sharding import Mesh
from jax.sharding import PartitionSpec as P

HEADS = 64
KVH = 8
PMAX = 64
BLK = 16

NY, NW, NX, NH, NC = 4, 4, 4, 8, 2


def run_pairs(moves):
    pairs = []
    for w in range(NW):
        for sh, sc, shift, th, tc in moves:
            source = (w * NH + sh) * NC + sc
            target = ((w + shift) % NW * NH + th) * NC + tc
            pairs.append((source, target))
    return pairs


FORWARD_FAR = [(6 + d // 2, d % 2, 2, d, 0) for d in range(4)] + [
    (d // 2 - 2, d % 2, 2, d, 0) for d in range(4, 8)
]
FORWARD_NEXT = [(2 + d // 2, 1 - d % 2, 1, d, 1) for d in range(8)]
FORWARD_BACK = [(d // 2, d % 2, -1, d, 1) for d in range(8)]
BACKWARD_FAR = [(d, 0, 2, d, 0) for d in range(8)]
BACKWARD_NEXT = [(d, 1, 1, d, 1) for d in range(8)]
BACKWARD_BACK = [(d, 1, -1, d, 1) for d in range(8)]
RUN = ("w", "h", "c")
SWAP = [(0, 1), (1, 0)]


def head_table(moves):
    table = [0] * (NH * NC)
    for sh, sc, _, th, _ in moves:
        table[sh * NC + sc] = th
    return jnp.array(table, jnp.int32)


def coordinates(bin_index):
    return bin_index // (NW * NX), bin_index // NX % NW, bin_index % NX


def body(queries, keys_values, grad_out, segments, partner, prompt_blocks):
    rows_here = queries.shape[0]
    heads_here = queries.shape[1]
    head_dim = queries.shape[2]
    score_scaling = 1.0 / math.sqrt(head_dim)
    y, w, x = lax.axis_index("y"), lax.axis_index("w"), lax.axis_index("x")
    h, c = lax.axis_index("h"), lax.axis_index("c")
    self_index = (y * NW + w) * NX + x
    bin_ids = jnp.arange(NY * NW * NX, dtype=jnp.int32)
    inverse = jnp.sum(jnp.where(partner[None, :] == bin_ids[:, None], bin_ids[None, :], 0), axis=1)
    owner_bin = partner[self_index]
    yo, wo, xo = coordinates(owner_bin)

    prompts = keys_values[:PMAX]
    mine = h * NC + c

    def prompt_of(head):
        return lax.dynamic_index_in_dim(prompts, head, 2, keepdims=False)

    far_or_next = lax.ppermute(
        prompt_of(head_table(FORWARD_FAR + FORWARD_NEXT)[mine]), RUN,
        run_pairs(FORWARD_FAR + FORWARD_NEXT),
    )
    back = lax.ppermute(prompt_of(head_table(FORWARD_BACK)[mine]), RUN, run_pairs(FORWARD_BACK))
    own = prompt_of(h)
    first = jnp.where(c == 0, own, back)
    second = far_or_next
    slots = jnp.arange(NY * NX, dtype=jnp.int32)
    slot_bins = (slots // NX * NW + w) * NX + slots % NX
    slot_rel = (coordinates(partner[slot_bins])[1] - w) % NW
    take_first = slot_rel < 2
    outgoing = jnp.where(take_first[:, None, None, None], first[None], second[None])
    incoming = lax.all_to_all(outgoing, ("y", "x"), split_axis=0, concat_axis=0, tiled=True)
    got = lax.dynamic_index_in_dim(incoming, yo * NX + xo, 0, keepdims=False)
    other = lax.ppermute(got, "c", SWAP)
    remote = jnp.where((wo - w) % 2 == c, got, other)

    kv_local = lax.dynamic_index_in_dim(keys_values, h, 2, keepdims=False)
    every_key_row = jnp.concatenate([kv_local[:, 0], remote[:, 0]], axis=0)
    every_value_row = jnp.concatenate([kv_local[:, 1], remote[:, 1]], axis=0)

    positions = jnp.arange(rows_here, dtype=jnp.int32)
    local_ok = (segments[:, None] == segments[None, :]) & (positions[None, :] <= positions[:, None])
    live_count = BLK * prompt_blocks[owner_bin]
    remote_ok = (segments[:, None] == 1) & (jnp.arange(PMAX, dtype=jnp.int32)[None, :] < live_count)
    allowed = jnp.concatenate([local_ok, remote_ok], axis=1)[None]
    score_matrix = (
        jnp.einsum("iwh,lh->wil", queries, every_key_row, preferred_element_type=jnp.float32)
        * score_scaling
    )
    score_matrix = jnp.where(allowed, score_matrix, -jnp.inf)
    row_peak = jnp.max(score_matrix, axis=-1, keepdims=True)
    weights_raw = jnp.where(allowed, jnp.exp(score_matrix - row_peak), jnp.float32(0.0))
    probabilities = weights_raw / jnp.sum(weights_raw, axis=-1, keepdims=True)
    probability_lowprec = probabilities.astype(jnp.bfloat16)
    attention = jnp.einsum(
        "qiu,ux->iqx", probability_lowprec, every_value_row, preferred_element_type=jnp.float32
    ).astype(jnp.bfloat16)
    row_delta = jnp.sum(grad_out.astype(jnp.float32) * attention.astype(jnp.float32), axis=-1)
    row_delta = jnp.transpose(row_delta, (1, 0))
    probability_gradient = jnp.einsum(
        "iwh,lh->wil", grad_out, every_value_row, preferred_element_type=jnp.float32
    )
    score_gradient = (probabilities * (probability_gradient - row_delta[..., None])).astype(
        jnp.bfloat16
    )
    query_gradient = (
        jnp.einsum("qiu,ux->iqx", score_gradient, every_key_row, preferred_element_type=jnp.float32)
        * score_scaling
    ).astype(jnp.bfloat16)
    key_grad = (
        jnp.einsum("mox,omn->xn", score_gradient, queries, preferred_element_type=jnp.float32)
        * score_scaling
    )
    value_grad = jnp.einsum(
        "mox,omn->xn", probability_lowprec, grad_out, preferred_element_type=jnp.float32
    )
    kv_grads = jnp.stack([key_grad, value_grad], axis=0).astype(jnp.bfloat16)
    local_part = kv_grads[:, :rows_here]
    remote_part = kv_grads[:, rows_here:]

    remote_total = (
        remote_part.astype(jnp.float32) + lax.ppermute(remote_part, "c", SWAP).astype(jnp.float32)
    ).astype(jnp.bfloat16)
    spread = lax.all_to_all(
        jnp.broadcast_to(remote_total[None], (NY * NX, *remote_total.shape)),
        ("y", "x"), split_axis=0, concat_axis=0, tiled=True,
    )

    def parcel_for(shift):
        target = (y * NW + (w + shift) % NW) * NX + x
        yr, _, xr = coordinates(inverse[target])
        return lax.dynamic_index_in_dim(spread, yr * NX + xr, 0, keepdims=False)

    far_or_next_back = lax.ppermute(
        parcel_for(jnp.where(c == 0, 2, 1)), RUN, run_pairs(BACKWARD_FAR + BACKWARD_NEXT)
    )
    back_back = lax.ppermute(parcel_for(-1), RUN, run_pairs(BACKWARD_BACK))
    stay = parcel_for(0)
    rel = (coordinates(inverse[self_index])[1] - w) % NW
    arrived = jnp.where(c == 0, stay, back_back)
    arrived = jnp.where(rel < 2, arrived, far_or_next_back)
    arrived = jnp.where(rel % 2 == c, arrived, jnp.zeros((), arrived.dtype))
    kept = lax.dynamic_index_in_dim(local_part, c, 0, keepdims=False)
    given = lax.dynamic_index_in_dim(local_part, 1 - c, 0, keepdims=False)
    kept_prompt = lax.dynamic_index_in_dim(arrived, c, 0, keepdims=False)
    given_prompt = lax.dynamic_index_in_dim(arrived, 1 - c, 0, keepdims=False)
    swapped = lax.ppermute(given, "c", SWAP)
    swapped_prompt = lax.ppermute(given_prompt, "c", SWAP)
    own_sum = kept.astype(jnp.float32) + swapped.astype(jnp.float32)
    prompt_rows = (
        own_sum[:PMAX] + kept_prompt.astype(jnp.float32) + swapped_prompt.astype(jnp.float32)
    )
    kv_result = jnp.concatenate([prompt_rows, own_sum[PMAX:]], axis=0).astype(jnp.bfloat16)
    return (attention, query_gradient, kv_result)


def solution(mesh):
    fine = Mesh(mesh.devices.reshape(NY, NW, NX, NH, NC), ("y", "w", "x", "h", "c"))
    seq, head = ("y", "w", "x"), ("h", "c")
    in_specs = (
        P(seq, head, None),
        P(seq, None, None, None),
        P(seq, head, None),
        P(seq),
        P(),
        P(),
    )
    out_specs = (P(seq, head, None), P(seq, head, None), P(seq, head))
    return jax.shard_map(body, mesh=fine, in_specs=in_specs, out_specs=out_specs, check_vma=False)
```

time: 442 us -> 140 us (0.32)
  the two profiles are of different devices: /device:TPU:97 before, /device:TPU:1 now
where the time goes in v1:
time: 140 us; the launch traced here: 139 us
  starting transfers between devices  69.6 us (50%)
  between operations  20.1 us (14%)
  local copies, waits for them, and re-layouts  16.6 us (12%)
  matrix products  12.1 us (9%)
  other arithmetic  10.8 us (8%)
  waiting for transfers between devices  9.66 us (7%)
    ppermute x1, starting transfers between devices, body(): lax.ppermute(prompt_of(head_table(FORWARD_FAR + FORWARD_NEXT)[mine]), RUN...  26.6 us
    ppermute x1, starting transfers between devices, body(): lax.ppermute(parcel_for(jnp.where(c == 0, 2, 1)), RUN, run_pairs(BACKWARD...  8.45 us
    ppermute x1, starting transfers between devices, body(): swapped_prompt = lax.ppermute(given_prompt, 'c', SWAP)  6.95 us
    all_to_all x1, starting transfers between devices, body(): lax.all_to_all(outgoing, ('y', 'x'), split_axis=0, concat_axis=0, tiled=T...  6.75 us
    all_to_all x1, waiting for transfers between devices, body(): lax.all_to_all(outgoing, ('y', 'x'), split_axis=0, concat_axis=0, tiled=T...  5.77 us
    ppermute x1, starting transfers between devices, body(): back_back = lax.ppermute(parcel_for(-1), RUN, run_pairs(BACKWARD_BACK))  5.54 us
    ppermute x1, starting transfers between devices, body(): lax.ppermute(prompt_of(head_table(FORWARD_BACK)[mine]), RUN, run_pairs(FO...  5.17 us
    sub x1, matrix products, body(): score_matrix - row_peak  4.89 us
  transfers between devices with their start and end apart: 10, of which 4 were waited for; matrix products, arithmetic and copies ran while one was open for 13% of the time, Pallas kernels for 0%

profile of v1, /device:TPU:1, one launch (start us, length us, event | category | flops | bytes accessed | tf_op | source)
XLA Modules:
  0.0 138.9 jit_solution(12340778457438607512)
XLA Ops:
  0.7 1.3 dynamic_slice.69
  3.3 1.2 dynamic_slice.71
  8.3 26.6 %collective-permute-start.1 = (bf16[64,2,128]{2,0,1:T(8,128)(2,1)S(1)}, bf16[64,2,128]{2,0,1:T(8,128)(2,1)S(1)}, u32[]{:S(2)}, u32[]{:S(2)}) collective-permute-start(bf16[64,2,128]{2,0,1:T(8,128)(2,1)S(1)} %bitcast.121), channel_id=1, source_target_pairs={{12,128},{13,130},{14,132},{15,134},{0,136},{1,138},{2,140},{3,142... | collective-permute-start | bytes 98312 | tf_op jit(solution)/shard_map/ppermute | solution.py:69
  35.0 5.2 %collective-permute-start = (bf16[64,2,128]{2,0,1:T(8,128)(2,1)S(1)}, bf16[64,2,128]{2,0,1:T(8,128)(2,1)S(1)}, u32[]{:S(2)}, u32[]{:S(2)}) collective-permute-start(bf16[64,2,128]{2,0,1:T(8,128)(2,1)S(1)} %bitcast.122), channel_id=1, source_target_pairs={{0,193},{1,195},{2,197},{3,199},{4,201},{5,203},{6,205},{7,207},{6... | collective-permute-start | bytes 98312 | tf_op jit(solution)/shard_map/ppermute | solution.py:73
  46.0 1.3 gather_fusion
  47.5 1.8 %collective-permute-done = bf16[64,2,128]{2,0,1:T(8,128)(2,1)S(1)} collective-permute-done((bf16[64,2,128]{2,0,1:T(8,128)(2,1)S(1)}, bf16[64,2,128]{2,0,1:T(8,128)(2,1)S(1)}, u32[]{:S(2)}, u32[]{:S(2)}) %collective-permute-start) | collective-permute-done | bytes 32800 | tf_op jit(solution)/shard_map/ppermute | solution.py:73
  50.2 6.8 %all-to-all-start = ((bf16[16,64,2,128]{3,1,2,0:T(8,128)(2,1)}), bf16[16,64,2,128]{3,1,2,0:T(8,128)(2,1)S(1)}, u32[]{:S(2)}, u32[]{:S(2)}) async-start(bf16[16,64,2,128]{3,1,2,0:T(8,128)(2,1)} %broadcast_select_fusion), calls=%async_computation | async-start | bytes 1048576 | tf_op jit(solution)/shard_map/all_to_all | solution.py:82
  57.0 2.1 %constant_dynamic-slice_fusion.3 = bf16[512,2,1,128]{3,2,1,0:T(2,128)(2,1)S(1)} fusion(bf16[512,2,8,128]{3,2,1,0:T(8,128)(2,1)} %param.9, s32[]{:T(128)S(6)} %select_n.240), kind=kLoop, calls=%fused_computation.73 | loop fusion | bytes 524292 | tf_op jit(solution)/shard_map/jit(dynamic_index_in_dim)/dynamic_slice | solution.py:87
  61.4 5.8 %all-to-all-done = bf16[16,64,2,128]{3,1,2,0:T(8,128)(2,1)S(1)} async-done(((bf16[16,64,2,128]{3,1,2,0:T(8,128)(2,1)}), bf16[16,64,2,128]{3,1,2,0:T(8,128)(2,1)S(1)}, u32[]{:S(2)}, u32[]{:S(2)}) %all-to-all-start) | async-done | bytes 524320 | tf_op jit(solution)/shard_map/all_to_all | solution.py:82
  67.2 1.9 %collective-permute-start.2 = (bf16[64,2,128]{2,0,1:T(8,128)(2,1)S(1)}, bf16[64,2,128]{2,0,1:T(8,128)(2,1)S(1)}, u32[]{:S(2)}, u32[]{:S(2)}) collective-permute-start(bf16[64,2,128]{2,0,1:T(8,128)(2,1)S(1)} %dynamic-slice_bitcast_fusion.3), channel_id=1, source_target_pairs={{0,1},{1,0},{2,3},{3,2},{4,5},{5,4},{6,7},{7,6},{8,9},{9,8},{10,11... | collective-permute-start | bytes 98312 | tf_op jit(solution)/shard_map/ppermute | solution.py:84
  70.3 4.9 %fusion.52 = (f32[4,512]{1,0:T(4,128)}, f32[4,512,576]{1,2,0:T(8,128)}) fusion(pred[512,576]{0,1:T(8,128)(4,1)S(1)} %pad_add_fusion, bf16[512,4,128]{2,1,0:T(4,128)(2,1)S(1)} %copy-done, bf16[64,128]{1,0:T(8,128)(2,1)S(1)} %get-tuple-element.20, bf16[512,128]{1,0:T(8,128)(2,1)S(1)} %get-tuple-element.15), kind=kOutput, calls=%fused_computation.109 | convolution fusion | flops 308183616 | bytes 5693440 | tf_op jit(solution)/shard_map/sub | solution.py:102
  75.2 3.2 %fusion.7 = bf16[4,512,576]{1,2,0:T(8,128)(2,1)S(1)} fusion(f32[4,512,576]{1,2,0:T(8,128)} %get-tuple-element.26, f32[4,512]{1,0:T(4,128)} %get-tuple-element.25), kind=kLoop, calls=%fused_computation.12 | loop fusion | flops 2359296 | bytes 7086080 | tf_op jit(solution)/shard_map/convert_element_type | solution.py:104
  79.2 1.7 %multiply_reduce_fusion = (f32[512,4]{0,1:T(4,128)S(1)}, bf16[512,4,128]{0,2,1:T(8,128)(2,1)S(1)}) fusion(bf16[512,4,128]{0,2,1:T(8,128)(2,1)} %copy-done.2, bf16[4,512,576]{1,2,0:T(8,128)(2,1)S(1)} %fusion.7, bf16[64,128]{1,0:T(8,128)(2,1)S(1)} %get-tuple-element.19, bf16[512,128]{1,0:T(8,128)(2,1)S(1)} %get-tuple-element.14), kind=kOutput, calls=%fused_computation.26 | convolution fusion | flops 303593472 | bytes 3563520 | tf_op jit(solution)/shard_map/qiu,ux->iqx/dot_general | solution.py:105
  81.0 1.8 %fusion.2 = bf16[4,512,576]{1,2,0:T(8,128)(2,1)S(1)} fusion(f32[4,512]{1,0:T(4,128)S(1)} %bitcast.123, bf16[512,4,128]{0,2,1:T(8,128)(2,1)} %copy-done.2, f32[4,512,576]{1,2,0:T(8,128)S(1)} %bitcast.119, f32[4,512]{1,0:T(4,128)S(1)} %copy-done.10, bf16[64,128]{1,0:T(8,128)(2,1)S(1)} %get-tuple-element.19, bf16[512,128]{1,0:T(8,128)(2,1)S(1)} %get-tuple-element.14), kind=kOutput, calls=%fused_computation.4 | convolution fusion | flops 307003392 | bytes 7766016 | tf_op jit(solution)/shard_map/iwh,lh->wil/dot_general | solution.py:110
  84.3 2.1 %collective-permute-start.4 = (bf16[2,64,128]{2,1,0:T(8,128)(2,1)}, bf16[2,64,128]{2,1,0:T(8,128)(2,1)}, u32[]{:S(2)}, u32[]{:S(2)}) collective-permute-start(bf16[2,64,128]{2,1,0:T(8,128)(2,1)} %pad_maximum_fusion.1), channel_id=1, source_target_pairs={{0,1},{1,0},{2,3},{3,2},{4,5},{5,4},{6,7},{7,6},{8,9},{9,8},{10,11... | collective-permute-start | bytes 98312 | tf_op jit(solution)/shard_map/ppermute | solution.py:132
  86.4 1.3 collective-permute-done.4
  89.4 4.2 %all-to-all-start.1 = ((bf16[16,2,64,128]{3,2,1,0:T(8,128)(2,1)}), bf16[16,2,64,128]{3,2,1,0:T(8,128)(2,1)}, u32[]{:S(2)}, u32[]{:S(2)}) async-start(bf16[16,2,64,128]{3,2,1,0:T(8,128)(2,1)} %broadcast_in_dim.93), calls=%async_computation.1 | async-start | bytes 1048576 | tf_op jit(solution)/shard_map/all_to_all | solution.py:134
  104.9 1.7 %fusion.27 = bf16[2,512,128]{2,1,0:T(8,128)(2,1)} fusion(bf16[1,576,128]{2,1,0:T(8,128)(2,1)} %copy-done.4, bf16[1,576,128]{2,1,0:T(8,128)(2,1)} %copy-done.3), kind=kLoop, calls=%fused_computation.37 | loop fusion | flops 131072 | bytes 557056 | tf_op jit(solution)/shard_map/stack | solution.py:127
  106.6 2.1 %fusion.10 = bf16[512,4,128]{0,2,1:T(8,128)(2,1)} fusion(bf16[4,512,576]{1,2,0:T(8,128)(2,1)S(1)} %fusion.2, bf16[64,128]{1,0:T(8,128)(2,1)} %copy-done.8, bf16[512,128]{1,0:T(8,128)(2,1)S(1)} %copy-done.7), kind=kOutput, calls=%fused_computation.17 | convolution fusion | flops 302809088 | bytes 3031040 | tf_op jit(solution)/shard_map/qiu,ux->iqx/dot_general | solution.py:117
  109.5 5.5 %collective-permute-start.5 = (bf16[2,64,128]{2,1,0:T(8,128)(2,1)S(1)}, bf16[2,64,128]{2,1,0:T(8,128)(2,1)S(1)}, u32[]{:S(2)}, u32[]{:S(2)}) collective-permute-start(bf16[2,64,128]{2,1,0:T(8,128)(2,1)S(1)} %get-tuple-element.12), channel_id=1, source_target_pairs={{1,193},{3,195},{5,197},{7,199},{9,201},{11,203},{13,205},{15,207}... | collective-permute-start | bytes 98312 | tf_op jit(solution)/shard_map/ppermute | solution.py:147
  115.0 8.4 %collective-permute-start.6 = (bf16[2,64,128]{2,1,0:T(8,128)(2,1)S(1)}, bf16[2,64,128]{2,1,0:T(8,128)(2,1)S(1)}, u32[]{:S(2)}, u32[]{:S(2)}) collective-permute-start(bf16[2,64,128]{2,1,0:T(8,128)(2,1)S(1)} %get-tuple-element.13), channel_id=1, source_target_pairs={{0,128},{2,130},{4,132},{6,134},{8,136},{10,138},{12,140},{14,142}... | collective-permute-start | bytes 98312 | tf_op jit(solution)/shard_map/ppermute | solution.py:144
  124.4 2.1 %copy.36 = bf16[512,4,128]{2,1,0:T(4,128)(2,1)} copy(bf16[512,4,128]{0,2,1:T(8,128)(2,1)} %fusion.10) | data formatting | bytes 1048576
  126.5 1.9 %collective-permute-start.3 = (bf16[512,128]{1,0:T(8,128)(2,1)S(1)}, bf16[512,128]{1,0:T(8,128)(2,1)S(1)}, u32[]{:S(2)}, u32[]{:S(2)}) collective-permute-start(bf16[512,128]{1,0:T(8,128)(2,1)S(1)} %dynamic-slice_bitcast_fusion), channel_id=1, source_target_pairs={{0,1},{1,0},{2,3},{3,2},{4,5},{5,4},{6,7},{7,6},{8,9},{9,8},{10,11... | collective-permute-start | bytes 393224 | tf_op jit(solution)/shard_map/ppermute | solution.py:157
  130.3 6.9 %collective-permute-start.7 = (bf16[64,128]{1,0:T(8,128)(2,1)S(1)}, bf16[64,128]{1,0:T(8,128)(2,1)S(1)}, u32[]{:S(2)}, u32[]{:S(2)}) collective-permute-start(bf16[64,128]{1,0:T(8,128)(2,1)S(1)} %dynamic-slice_bitcast_fusion.4), channel_id=1, source_target_pairs={{0,1},{1,0},{2,3},{3,2},{4,5},{5,4},{6,7},{7,6},{8,9},{9,8},{10,11... | collective-permute-start | bytes 49160 | tf_op jit(solution)/shard_map/ppermute | solution.py:158
  (72 shorter events, 16.7 us)
Async XLA Ops:
  0.6 69.7 %copy-start = (bf16[512,4,128]{2,1,0:T(4,128)(2,1)S(1)}, bf16[512,4,128]{2,1,0:T(4,128)(2,1)}, u32[]{:S(2)}) copy-start(bf16[512,4,128]{2,1,0:T(4,128)(2,1)} %param.8) | copy-start | bytes 1572868
  0.6 60.5 %copy-start.9 = (s32[512]{0:T(512)S(1)}, s32[512]{0:T(512)}, u32[]{:S(2)}) copy-start(s32[512]{0:T(512)} %param.11) | copy-start | bytes 6148
  0.7 68.5 %copy-start.5 = (bf16[512,4,128]{2,1,0:T(4,128)(2,1)S(1)}, bf16[512,4,128]{2,1,0:T(4,128)(2,1)}, u32[]{:S(2)}) copy-start(bf16[512,4,128]{2,1,0:T(4,128)(2,1)} %param.10) | copy-start | bytes 1572868
  8.3 41.0 %collective-permute-start.1 = (bf16[64,2,128]{2,0,1:T(8,128)(2,1)S(1)}, bf16[64,2,128]{2,0,1:T(8,128)(2,1)S(1)}, u32[]{:S(2)}, u32[]{:S(2)}) collective-permute-start(bf16[64,2,128]{2,0,1:T(8,128)(2,1)S(1)} %bitcast.121), channel_id=1, source_target_pairs={{12,128},{13,130},{14,132},{15,134},{0,136},{1,138},{2,140},{3,142... | collective-permute-start | bytes 98312 | tf_op jit(solution)/shard_map/ppermute | solution.py:69
  35.0 14.3 %collective-permute-start = (bf16[64,2,128]{2,0,1:T(8,128)(2,1)S(1)}, bf16[64,2,128]{2,0,1:T(8,128)(2,1)S(1)}, u32[]{:S(2)}, u32[]{:S(2)}) collective-permute-start(bf16[64,2,128]{2,0,1:T(8,128)(2,1)S(1)} %bitcast.122), channel_id=1, source_target_pairs={{0,193},{1,195},{2,197},{3,199},{4,201},{5,203},{6,205},{7,207},{6... | collective-permute-start | bytes 98312 | tf_op jit(solution)/shard_map/ppermute | solution.py:73
  50.2 17.0 %all-to-all-start = ((bf16[16,64,2,128]{3,1,2,0:T(8,128)(2,1)}), bf16[16,64,2,128]{3,1,2,0:T(8,128)(2,1)S(1)}, u32[]{:S(2)}, u32[]{:S(2)}) async-start(bf16[16,64,2,128]{3,1,2,0:T(8,128)(2,1)} %broadcast_select_fusion), calls=%async_computation | async-start | bytes 1048576 | tf_op jit(solution)/shard_map/all_to_all | solution.py:82
  61.4 13.8 %copy-start.6 = (bf16[512,128]{1,0:T(8,128)(2,1)}, bf16[512,128]{1,0:T(8,128)(2,1)S(1)}, u32[]{:S(2)}) copy-start(bf16[512,128]{1,0:T(8,128)(2,1)S(1)} %get-tuple-element.15) | copy-start | bytes 393220
  67.2 3.1 %collective-permute-start.2 = (bf16[64,2,128]{2,0,1:T(8,128)(2,1)S(1)}, bf16[64,2,128]{2,0,1:T(8,128)(2,1)S(1)}, u32[]{:S(2)}, u32[]{:S(2)}) collective-permute-start(bf16[64,2,128]{2,0,1:T(8,128)(2,1)S(1)} %dynamic-slice_bitcast_fusion.3), channel_id=1, source_target_pairs={{0,1},{1,0},{2,3},{3,2},{4,5},{5,4},{6,7},{7,6},{8,9},{9,8},{10,11... | collective-permute-start | bytes 98312 | tf_op jit(solution)/shard_map/ppermute | solution.py:84
  69.5 8.9 %copy-start.2 = (bf16[512,4,128]{0,2,1:T(8,128)(2,1)}, bf16[512,4,128]{0,2,1:T(8,128)(2,1)S(1)}, u32[]{:S(2)}) copy-start(bf16[512,4,128]{0,2,1:T(8,128)(2,1)S(1)} %copy.32) | copy-start | bytes 1572868
  70.3 4.9 %copy-start.8 = (bf16[64,128]{1,0:T(8,128)(2,1)}, bf16[64,128]{1,0:T(8,128)(2,1)S(1)}, u32[]{:S(2)}) copy-start(bf16[64,128]{1,0:T(8,128)(2,1)S(1)} %get-tuple-element.20) | copy-start | bytes 49156
  75.2 5.7 %slice-start = ((s8[4718592]{0:T(1024)(128)(4,1)}), s8[4194304]{0:T(1024)(128)(4,1)S(1)}, s32[]{:S(2)}) async-start(s8[4718592]{0:T(1024)(128)(4,1)} %bitcast.118), calls=%async_computation.2 | async-start | bytes 8388608
  78.4 2.5 %slice-start.1 = ((s8[4718592]{0:T(1024)(128)(4,1)}), s8[524288]{0:T(1024)(128)(4,1)S(1)}, s32[]{:S(2)}) async-start(s8[4718592]{0:T(1024)(128)(4,1)} %bitcast.118), calls=%async_computation.3 | async-start | bytes 1048576
  78.4 2.5 %copy-start.10 = (f32[4,512]{1,0:T(4,128)S(1)}, f32[4,512]{1,0:T(4,128)}, u32[]{:S(2)}) copy-start(f32[4,512]{1,0:T(4,128)} %get-tuple-element.25) | copy-start | bytes 24580
  79.2 4.4 %copy-start.3 = (bf16[1,576,128]{2,1,0:T(8,128)(2,1)}, bf16[1,576,128]{2,1,0:T(8,128)(2,1)S(1)}, u32[]{:S(2)}) copy-start(bf16[1,576,128]{2,1,0:T(8,128)(2,1)S(1)} %fusion.14) | copy-start | bytes 442372
  82.8 10.9 %copy-start.1 = (s32[64]{0:T(128)S(1)}, s32[64]{0:T(128)}, u32[]{:S(2)}) copy-start(s32[64]{0:T(128)} %param.12) | copy-start | bytes 772
  82.8 23.8 %copy-start.7 = (bf16[512,128]{1,0:T(8,128)(2,1)S(1)}, bf16[512,128]{1,0:T(8,128)(2,1)}, u32[]{:S(2)}) copy-start(bf16[512,128]{1,0:T(8,128)(2,1)} %copy-done.6) | copy-start | bytes 393220
  83.6 0.7 copy-start.4
  84.3 3.4 %collective-permute-start.4 = (bf16[2,64,128]{2,1,0:T(8,128)(2,1)}, bf16[2,64,128]{2,1,0:T(8,128)(2,1)}, u32[]{:S(2)}, u32[]{:S(2)}) collective-permute-start(bf16[2,64,128]{2,1,0:T(8,128)(2,1)} %pad_maximum_fusion.1), channel_id=1, source_target_pairs={{0,1},{1,0},{2,3},{3,2},{4,5},{5,4},{6,7},{7,6},{8,9},{9,8},{10,11... | collective-permute-start | bytes 98312 | tf_op jit(solution)/shard_map/ppermute | solution.py:132
  89.4 19.3 %all-to-all-start.1 = ((bf16[16,2,64,128]{3,2,1,0:T(8,128)(2,1)}), bf16[16,2,64,128]{3,2,1,0:T(8,128)(2,1)}, u32[]{:S(2)}, u32[]{:S(2)}) async-start(bf16[16,2,64,128]{3,2,1,0:T(8,128)(2,1)} %broadcast_in_dim.93), calls=%async_computation.1 | async-start | bytes 1048576 | tf_op jit(solution)/shard_map/all_to_all | solution.py:134
  109.5 20.0 %collective-permute-start.5 = (bf16[2,64,128]{2,1,0:T(8,128)(2,1)S(1)}, bf16[2,64,128]{2,1,0:T(8,128)(2,1)S(1)}, u32[]{:S(2)}, u32[]{:S(2)}) collective-permute-start(bf16[2,64,128]{2,1,0:T(8,128)(2,1)S(1)} %get-tuple-element.12), channel_id=1, source_target_pairs={{1,193},{3,195},{5,197},{7,199},{9,201},{11,203},{13,205},{15,207}... | collective-permute-start | bytes 98312 | tf_op jit(solution)/shard_map/ppermute | solution.py:147
  115.0 14.5 %collective-permute-start.6 = (bf16[2,64,128]{2,1,0:T(8,128)(2,1)S(1)}, bf16[2,64,128]{2,1,0:T(8,128)(2,1)S(1)}, u32[]{:S(2)}, u32[]{:S(2)}) collective-permute-start(bf16[2,64,128]{2,1,0:T(8,128)(2,1)S(1)} %get-tuple-element.13), channel_id=1, source_target_pairs={{0,128},{2,130},{4,132},{6,134},{8,136},{10,138},{12,140},{14,142}... | collective-permute-start | bytes 98312 | tf_op jit(solution)/shard_map/ppermute | solution.py:144
  126.5 10.7 %collective-permute-start.3 = (bf16[512,128]{1,0:T(8,128)(2,1)S(1)}, bf16[512,128]{1,0:T(8,128)(2,1)S(1)}, u32[]{:S(2)}, u32[]{:S(2)}) collective-permute-start(bf16[512,128]{1,0:T(8,128)(2,1)S(1)} %dynamic-slice_bitcast_fusion), channel_id=1, source_target_pairs={{0,1},{1,0},{2,3},{3,2},{4,5},{5,4},{6,7},{7,6},{8,9},{9,8},{10,11... | collective-permute-start | bytes 393224 | tf_op jit(solution)/shard_map/ppermute | solution.py:157
  130.3 7.9 %collective-permute-start.7 = (bf16[64,128]{1,0:T(8,128)(2,1)S(1)}, bf16[64,128]{1,0:T(8,128)(2,1)S(1)}, u32[]{:S(2)}, u32[]{:S(2)}) collective-permute-start(bf16[64,128]{1,0:T(8,128)(2,1)S(1)} %dynamic-slice_bitcast_fusion.4), channel_id=1, source_target_pairs={{0,1},{1,0},{2,3},{3,2},{4,5},{5,4},{6,7},{7,6},{8,9},{9,8},{10,11... | collective-permute-start | bytes 49160 | tf_op jit(solution)/shard_map/ppermute | solution.py:158

commit v2 on v1

v2 whole, which is shorter than its diff:
```python
import math

import jax
import jax.numpy as jnp
from jax import lax
from jax.experimental import pallas as pl
from jax.experimental.pallas import tpu as pltpu
from jax.sharding import Mesh
from jax.sharding import PartitionSpec as P

HEADS = 64
KVH = 8
PMAX = 64
BLK = 16

NY, NW, NX, NH, NC = 4, 4, 4, 8, 2


def run_pairs(moves):
    pairs = []
    for w in range(NW):
        for sh, sc, shift, th, tc in moves:
            source = (w * NH + sh) * NC + sc
            target = ((w + shift) % NW * NH + th) * NC + tc
            pairs.append((source, target))
    return pairs


FORWARD_FAR = [(6 + d // 2, d % 2, 2, d, 0) for d in range(4)] + [
    (d // 2 - 2, d % 2, 2, d, 0) for d in range(4, 8)
]
FORWARD_NEXT = [(2 + d // 2, 1 - d % 2, 1, d, 1) for d in range(8)]
FORWARD_BACK = [(d // 2, d % 2, -1, d, 1) for d in range(8)]
BACKWARD_FAR = [(d, 0, 2, d, 0) for d in range(8)]
BACKWARD_NEXT = [(d, 1, 1, d, 1) for d in range(8)]
BACKWARD_BACK = [(d, 1, -1, d, 1) for d in range(8)]
RUN = ("w", "h", "c")
SWAP = [(0, 1), (1, 0)]


SCALE = 1.0 / math.sqrt(128)
LOG_SCALE = SCALE * math.log2(math.e)
MASKED = -1e30
QROWS = 512
PROWS = 256
TILE = 128


LOW, HIGH, LIVE, DIRECT, CORE, SLOT, FIRST, SEND_FAR, SEND_BACK, SEND_STAY, ARRIVAL = range(11)


def route(partner_ref, blocks_ref, segments_ref, table_ref):
    y, w, x = lax.axis_index("y"), lax.axis_index("w"), lax.axis_index("x")
    c = lax.axis_index("c")
    here = y * 16 + w * 4 + x
    owner = partner_ref[here]
    owner_w = (owner >> 2) & 3

    def seek(index, carry):
        far, back, stay, responder = carry
        mark = partner_ref[index]
        shift = (((mark >> 2) & 3) - w) & 3
        in_column = ((mark >> 4) == y) & ((mark & 3) == x)
        slot = ((index >> 4) << 2) | (index & 3)
        far = jnp.where(in_column & (shift == jnp.where(c == 0, 2, 1)), slot, far)
        back = jnp.where(in_column & (shift == 3), slot, back)
        stay = jnp.where(in_column & (shift == 0), slot, stay)
        return far, back, stay, jnp.where(mark == here, index, responder)

    zero = jnp.int32(0)
    far, back, stay, responder = lax.fori_loop(
        0, NY * NW * NX, seek, (zero, zero, zero, zero), unroll=8
    )
    first = zero
    for slot in range(NY * NX):
        wanted = partner_ref[(slot // NX) * 16 + w * 4 + slot % NX]
        first = first | jnp.where((((wanted >> 2) & 3) - w) & 3 < 2, 1 << slot, 0)
    segments = segments_ref[...]
    first_token = jnp.sum((segments < 1).astype(jnp.float32)).astype(jnp.int32)
    end_token = jnp.sum((segments < 2).astype(jnp.float32)).astype(jnp.int32)
    rel = (((responder >> 2) & 3) - w) & 3
    table_ref[LOW] = first_token >> 6
    table_ref[HIGH] = (end_token + 63) >> 6
    table_ref[LIVE] = BLK * blocks_ref[owner]
    table_ref[DIRECT] = (((owner_w - w) & 1) == c).astype(jnp.int32)
    table_ref[CORE] = c
    table_ref[SLOT] = ((owner >> 4) << 2) | (owner & 3)
    table_ref[FIRST] = first
    table_ref[SEND_FAR] = far
    table_ref[SEND_BACK] = back
    table_ref[SEND_STAY] = stay
    table_ref[ARRIVAL] = jnp.where((rel & 1) == c, jnp.where(rel < 2, 1, 2), 0)


def dot(left, right, left_dim, right_dim):
    return lax.dot_general(
        left, right, (((left_dim,), (right_dim,)), ((), ())), preferred_element_type=jnp.float32
    )


def local_scores(q, gate, keys, key_segments, step):
    width = TILE * (step + 1)
    scores = dot(q, keys[:width], 1, 1) + dot(gate, key_segments[:width], 1, 1)
    shape = (QROWS, TILE)
    token = lax.broadcasted_iota(jnp.int32, shape, 0) // 4
    causal = lax.broadcasted_iota(jnp.int32, shape, 1) <= token
    last = jnp.where(causal, scores[:, width - TILE :], MASKED)
    if step == 0:
        return last
    return jnp.concatenate([scores[:, : width - TILE], last], axis=1)


def local_forward(q_ref, gate_ref, kv_ref, keyseg_ref, out_ref, lse_ref):
    for step in range(4):
        rows = pl.ds(step * QROWS, QROWS)
        width = TILE * (step + 1)
        scores = local_scores(q_ref[rows, :], gate_ref[rows, :], kv_ref[0], keyseg_ref[...], step)
        peak = jnp.max(scores, axis=1, keepdims=True)
        weights = jnp.exp2((scores - peak) * LOG_SCALE)
        total = jnp.sum(weights, axis=1, keepdims=True)
        mixed = dot(weights.astype(jnp.bfloat16), kv_ref[1, :width, :], 1, 0)
        out_ref[rows, :] = mixed / total
        lse_ref[rows, :] = jnp.broadcast_to(peak * LOG_SCALE + jnp.log2(total), (QROWS, TILE))


def pick(scalars_ref, got_ref, other_ref):
    return jnp.where(scalars_ref[DIRECT] == 1, got_ref[...], other_ref[...])


def prompt_step(
    scalars_ref, q_ref, grad_ref, gate_ref, got_ref, other_ref, outin_ref, lsein_ref,
    out_ref, lse_ref, dscore_ref, dprompt_ref, dkey_ref, dvalue_ref,
):
    index = pl.program_id(0)

    @pl.when(index == 0)
    def _():
        dkey_ref[...] = jnp.zeros_like(dkey_ref)
        dvalue_ref[...] = jnp.zeros_like(dvalue_ref)

    @pl.when((scalars_ref[LOW] <= index) & (index < scalars_ref[HIGH]))
    def _():
        prompt = pick(scalars_ref, got_ref, other_ref)
        keys, values = prompt[:PMAX], prompt[PMAX:]
        segment_one = (lax.broadcasted_iota(jnp.int32, (PMAX, TILE), 1) == 1).astype(jnp.bfloat16)
        alive = lax.broadcasted_iota(jnp.int32, (PROWS, PMAX), 1) < scalars_ref[LIVE]
        q, grad = q_ref[...], grad_ref[...]
        scores = dot(q, keys, 1, 1) + dot(gate_ref[...], segment_one, 1, 1)
        logits = jnp.where(alive, scores, MASKED) * LOG_SCALE
        lse = lsein_ref[:, :1]
        peak = jnp.maximum(lse, jnp.max(logits, axis=1, keepdims=True))
        weights = jnp.exp2(logits - peak)
        before = jnp.exp2(lse - peak)
        total = before + jnp.sum(weights, axis=1, keepdims=True)
        inverse = 1.0 / total
        probabilities = weights * inverse
        low = probabilities.astype(jnp.bfloat16)
        out = outin_ref[...] * (before * inverse) + dot(low, values, 1, 0)
        out_ref[...] = out
        lse_ref[...] = jnp.broadcast_to(peak + jnp.log2(total), (PROWS, TILE))
        rounded = out.astype(jnp.bfloat16).astype(jnp.float32)
        delta = jnp.sum(grad.astype(jnp.float32) * rounded, axis=1, keepdims=True)
        dscore = (probabilities * (dot(grad, values, 1, 1) - delta)).astype(jnp.bfloat16)
        dscore_ref[...] = dscore
        dvalue_ref[...] += dot(low, grad, 0, 0)
        dkey_ref[...] += dot(dscore, q, 0, 0)

    @pl.when(index == pl.num_programs(0) - 1)
    def _():
        dprompt_ref[:PMAX, :] = (dkey_ref[...] * SCALE).astype(jnp.bfloat16)
        dprompt_ref[PMAX:, :] = dvalue_ref[...].astype(jnp.bfloat16)


def local_backward(
    scalars_ref, q_ref, grad_ref, gate_ref, kv_ref, keyseg_ref, got_ref, other_ref,
    outlocal_ref, lselocal_ref, outprompt_ref, lseprompt_ref, dscore_ref,
    attention_ref, dquery_ref, kept_ref, given_ref, dkey_ref, dvalue_ref, acc_ref,
):
    def chosen(prompt_ref, local_ref, step):
        parts = []
        for part in range(QROWS // PROWS):
            index = step * (QROWS // PROWS) + part
            inside = (scalars_ref[LOW] <= index) & (index < scalars_ref[HIGH])
            rows = pl.ds(index * PROWS, PROWS)
            parts.append(jnp.where(inside, prompt_ref[rows, :], local_ref[rows, :]))
        return jnp.concatenate(parts, axis=0)

    dkey_ref[...] = jnp.zeros_like(dkey_ref)
    dvalue_ref[...] = jnp.zeros_like(dvalue_ref)
    prompt_keys = pick(scalars_ref, got_ref, other_ref)[:PMAX]
    for step in range(4):
        rows = pl.ds(step * QROWS, QROWS)
        width = TILE * (step + 1)
        q, grad = q_ref[rows, :], grad_ref[rows, :]
        attention = chosen(outprompt_ref, outlocal_ref, step).astype(jnp.bfloat16)
        attention_ref[rows, :] = attention
        delta = jnp.sum(
            grad.astype(jnp.float32) * attention.astype(jnp.float32), axis=1, keepdims=True
        )
        scores = local_scores(q, gate_ref[rows, :], kv_ref[0], keyseg_ref[...], step)
        lse = chosen(lseprompt_ref, lselocal_ref, step)
        if step:
            lse = jnp.concatenate([lse] * (step + 1), axis=1)
        probabilities = jnp.exp2(scores * LOG_SCALE - lse)
        low = probabilities.astype(jnp.bfloat16)
        dprob = dot(grad, kv_ref[1, :width, :], 1, 1)
        dscore = (probabilities * (dprob - delta)).astype(jnp.bfloat16)
        acc_ref[...] = dot(dscore, kv_ref[0, :width, :], 1, 0)
        dvalue_ref[:width, :] += dot(low, grad, 0, 0)
        dkey_ref[:width, :] += dot(dscore, q, 0, 0)
        for part in range(QROWS // PROWS):
            index = step * (QROWS // PROWS) + part

            @pl.when((scalars_ref[LOW] <= index) & (index < scalars_ref[HIGH]))
            def _():
                acc_ref[pl.ds(part * PROWS, PROWS), :] += dot(
                    dscore_ref[pl.ds(index * PROWS, PROWS), :], prompt_keys, 1, 0
                )

        dquery_ref[rows, :] = (acc_ref[...] * SCALE).astype(jnp.bfloat16)
    dkey = dkey_ref[...] * SCALE
    dvalue = dvalue_ref[...]
    keep_key = scalars_ref[CORE] == 0
    kept_ref[...] = jnp.where(keep_key, dkey, dvalue).astype(jnp.bfloat16)
    given_ref[...] = jnp.where(keep_key, dvalue, dkey).astype(jnp.bfloat16)


SMEM = pl.BlockSpec(memory_space=pltpu.SMEM)
VMEM = pl.BlockSpec(memory_space=pltpu.VMEM)


def body(queries, keys_values, grad_out, segments, partner, prompt_blocks):
    rows_here = queries.shape[0]
    heads_here = queries.shape[1]
    head_dim = queries.shape[2]
    flat = rows_here * heads_here
    y, w, x = lax.axis_index("y"), lax.axis_index("w"), lax.axis_index("x")
    h, c = lax.axis_index("h"), lax.axis_index("c")

    zero = jnp.uint32(0)

    def prompt_of(head):
        rows = lax.dynamic_slice(
            keys_values, (zero, zero, head.astype(jnp.uint32), zero), (PMAX, 2, 1, head_dim)
        )
        return jnp.transpose(rows[:, :, 0], (1, 0, 2)).reshape(2 * PMAX, head_dim)

    far_sender = (h < 2) | (h >= 6)
    head_far = jnp.where(h < 2, 2 * h + c + 4, 2 * h + c - 12)
    head_next = 2 * h + 1 - c - 4
    far_or_next = lax.ppermute(
        prompt_of(jnp.where(far_sender, head_far, head_next)), RUN,
        run_pairs(FORWARD_FAR + FORWARD_NEXT),
    )
    back = lax.ppermute(
        prompt_of((2 * h + c) & (NH - 1)), RUN, run_pairs(FORWARD_BACK)
    )
    own = prompt_of(h)

    table = pl.pallas_call(
        route, out_shape=jax.ShapeDtypeStruct((16,), jnp.int32), name="route",
        in_specs=[SMEM, SMEM, VMEM], out_specs=SMEM,
    )(partner, prompt_blocks, segments.reshape(-1, TILE))

    kv_local = jnp.transpose(
        lax.dynamic_index_in_dim(keys_values, h.astype(jnp.uint32), 2, keepdims=False), (1, 0, 2)
    )
    lanes = jnp.arange(TILE, dtype=jnp.int32)
    row_segments = jnp.broadcast_to(segments[:, None], (rows_here, heads_here)).reshape(flat)
    gate = jnp.where(row_segments[:, None] == lanes[None, :], 0.0, MASKED).astype(jnp.bfloat16)
    key_segments = (segments[:, None] == lanes[None, :]).astype(jnp.bfloat16)
    q = queries.reshape(flat, head_dim)
    grad = grad_out.reshape(flat, head_dim)

    wide = jax.ShapeDtypeStruct((flat, head_dim), jnp.float32)
    narrow = jax.ShapeDtypeStruct((flat, head_dim), jnp.bfloat16)
    prompt_shape = jax.ShapeDtypeStruct((2 * PMAX, head_dim), jnp.bfloat16)
    part_shape = jax.ShapeDtypeStruct((rows_here, head_dim), jnp.bfloat16)
    local_out, local_lse = pl.pallas_call(
        local_forward, out_shape=(wide, wide), name="local_forward",
        in_specs=[VMEM] * 4, out_specs=(VMEM, VMEM),
    )(q, gate, kv_local, key_segments)
    scalar = [table[k].astype(jnp.uint32) for k in range(11)]

    slots = jnp.arange(NY * NX, dtype=jnp.uint32)
    first = jnp.where(c == 0, own, back)
    take_first = (scalar[FIRST] >> slots) & 1 == 1
    outgoing = jnp.where(take_first[:, None, None], first[None], far_or_next[None])
    outgoing, local_out, local_lse, scalar = lax.optimization_barrier(
        (outgoing, local_out, local_lse, scalar)
    )
    incoming = lax.all_to_all(outgoing, ("y", "x"), split_axis=0, concat_axis=0, tiled=True)
    got = lax.dynamic_index_in_dim(incoming, scalar[SLOT], 0, keepdims=False)
    other = lax.ppermute(got, "c", SWAP)

    def rows_block(index, table_ref):
        return jnp.clip(index, table_ref[LOW], table_ref[HIGH] - 1), 0

    def whole(index, table_ref):
        return 0, 0

    wide_block = pl.BlockSpec((PROWS, head_dim), rows_block)
    whole_block = pl.BlockSpec((2 * PMAX, head_dim), whole)
    out, lse, dscore, dprompt = pl.pallas_call(
        prompt_step,
        out_shape=(
            wide, wide, jax.ShapeDtypeStruct((flat, PMAX), jnp.bfloat16), prompt_shape,
        ),
        grid_spec=pltpu.PrefetchScalarGridSpec(
            num_scalar_prefetch=1,
            grid=(flat // PROWS,),
            in_specs=[wide_block] * 3 + [whole_block] * 2 + [wide_block] * 2,
            out_specs=(
                wide_block, wide_block, pl.BlockSpec((PROWS, PMAX), rows_block), whole_block,
            ),
            scratch_shapes=[pltpu.VMEM((PMAX, head_dim), jnp.float32)] * 2,
        ),
        name="prompt_step",
    )(table, q, grad, gate, got, other, local_out, local_lse)

    total = dprompt.astype(jnp.float32) + lax.ppermute(dprompt, "c", SWAP).astype(jnp.float32)
    spread = jnp.where(
        (slots == scalar[SLOT])[:, None, None], total.astype(jnp.bfloat16)[None],
        jnp.zeros((), jnp.bfloat16),
    )
    spread = lax.all_to_all(spread, ("y", "x"), split_axis=0, concat_axis=0, tiled=True)

    def parcel(slot):
        return lax.dynamic_index_in_dim(spread, slot, 0, keepdims=False)

    far_or_next_back = lax.ppermute(
        parcel(scalar[SEND_FAR]), RUN, run_pairs(BACKWARD_FAR + BACKWARD_NEXT)
    )
    back_back = lax.ppermute(parcel(scalar[SEND_BACK]), RUN, run_pairs(BACKWARD_BACK))
    stay = parcel(scalar[SEND_STAY])

    attention, query_gradient, kept, given = pl.pallas_call(
        local_backward,
        out_shape=(narrow, narrow, part_shape, part_shape),
        name="local_backward",
        in_specs=[SMEM] + [VMEM] * 12,
        out_specs=(VMEM,) * 4,
        scratch_shapes=[pltpu.VMEM((rows_here, head_dim), jnp.float32)] * 3,
    )(
        table, q, grad, gate, kv_local, key_segments, got, other,
        local_out, local_lse, out, lse, dscore,
    )
    swapped = lax.ppermute(given, "c", SWAP)
    own_sum = kept.astype(jnp.float32) + swapped.astype(jnp.float32)

    arrived = jnp.where(c == 0, stay, back_back)
    arrived = jnp.where(scalar[ARRIVAL] == 2, far_or_next_back, arrived)
    arrived = jnp.where(scalar[ARRIVAL] == 0, jnp.zeros((), arrived.dtype), arrived)
    keep_row = (c * PMAX).astype(jnp.uint32)
    kept_prompt = lax.dynamic_slice(arrived, (keep_row, zero), (PMAX, head_dim))
    given_prompt = lax.dynamic_slice(arrived, (PMAX - keep_row, zero), (PMAX, head_dim))
    swapped_prompt = lax.ppermute(given_prompt, "c", SWAP)
    prompt_rows = (
        own_sum[:PMAX] + kept_prompt.astype(jnp.float32) + swapped_prompt.astype(jnp.float32)
    )
    kv_result = lax.dynamic_update_slice(
        own_sum.astype(jnp.bfloat16), prompt_rows.astype(jnp.bfloat16), (0, 0)
    )
    return (
        attention.reshape(queries.shape), query_gradient.reshape(queries.shape), kv_result
    )


def solution(mesh):
    fine = Mesh(mesh.devices.reshape(NY, NW, NX, NH, NC), ("y", "w", "x", "h", "c"))
    seq, head = ("y", "w", "x"), ("h", "c")
    in_specs = (
        P(seq, head, None),
        P(seq, None, None, None),
        P(seq, head, None),
        P(seq),
        P(),
        P(),
    )
    out_specs = (P(seq, head, None), P(seq, head, None), P(seq, head))
    return jax.shard_map(body, mesh=fine, in_specs=in_specs, out_specs=out_specs, check_vma=False)
```

time: 140 us -> 129 us (0.921)
  blocking collectives: 0 us -> 32.8 us
  Pallas kernels: 0 us -> 19.1 us
  between operations: 20.1 us -> 4.7 us
  starting transfers between devices: 69.6 us -> 56.8 us
  matrix products: 12.1 us -> 0 us
  local copies, waits for them, and re-layouts: 16.6 us -> 8.15 us
  waiting for transfers between devices: 9.66 us -> 1.89 us
  other arithmetic: 10.8 us -> 4.61 us
    all_to_all x0 -> x2, blocking collectives: none -> 32.8 us  [the longest x1 18.5 us: body(): lax.all_to_all(outgoing, ('y', 'x'), split_axis=0, concat_axis=0, tiled=T...]
    pallas_call x0 -> x4, Pallas kernels: none -> 19.1 us  [the longest x1 7.44 us: body(): pl.pallas_call(local_backward, out_shape=(narrow, narrow, part_shape, par...]
    all_to_all x2 -> x0, starting transfers between devices: 11 us -> none  [the longest x1 6.75 us: body(): lax.all_to_all(outgoing, ('y', 'x'), split_axis=0, concat_axis=0, tiled=T...]
    dot_general x5 -> x0, matrix products: 7.18 us -> none  [the longest x1 2.12 us: body(): jnp.einsum('qiu,ux->iqx', score_gradient, every_key_row, preferred_elemen...]
    all_to_all x2 -> x0, waiting for transfers between devices: 5.77 us -> none  [the longest x1 5.77 us: body(): lax.all_to_all(outgoing, ('y', 'x'), split_axis=0, concat_axis=0, tiled=T...]
    sub x1 -> x0, matrix products: 4.89 us -> none  [body(): score_matrix - row_peak]
    dynamic_slice x8 -> x4, local copies, waits for them, and re-layouts: 8.13 us -> 4.31 us  [the longest x2 2.91 us: body(): lax.dynamic_index_in_dim(keys_values, h.astype(jnp.uint32), 2, keepdims=F...]
    ppermute x1, starting transfers between devices: 6.95 us -> 4.19 us  [body(): swapped_prompt = lax.ppermute(given_prompt, 'c', SWAP)]
  transfers between devices with their start and end apart: 10 -> 8, of which waited for: 4 -> 2; matrix products, arithmetic and copies ran while one was open for 13% -> 7% of each run, Pallas kernels for 0% -> 11%
where the time goes in v2:
time: 129 us; the launch traced here: 128 us
  starting transfers between devices  56.8 us (44%)
  blocking collectives  32.8 us (25%)
  Pallas kernels  19.1 us (15%)
  local copies, waits for them, and re-layouts  8.15 us (6%)
  between operations  4.7 us (4%)
  other arithmetic  4.61 us (4%)
  waiting for transfers between devices  1.89 us (1%)
    ppermute x1, starting transfers between devices, body(): lax.ppermute(prompt_of(jnp.where(far_sender, head_far, head_next)), RUN,...  26.6 us
    all_to_all x1, blocking collectives, body(): lax.all_to_all(outgoing, ('y', 'x'), split_axis=0, concat_axis=0, tiled=T...  18.5 us
    all_to_all x1, blocking collectives, body(): lax.all_to_all(spread, ('y', 'x'), split_axis=0, concat_axis=0, tiled=True)  14.2 us
    ppermute x1, starting transfers between devices, body(): lax.ppermute(parcel(scalar[SEND_FAR]), RUN, run_pairs(BACKWARD_FAR + BACK...  7.63 us
    pallas_call x1, Pallas kernels, body(): pl.pallas_call(local_backward, out_shape=(narrow, narrow, part_shape, par...  7.44 us
    ppermute x1, starting transfers between devices, body(): lax.ppermute(parcel(scalar[SEND_BACK]), RUN, run_pairs(BACKWARD_BACK))  6.36 us
    ppermute x1, starting transfers between devices, body(): lax.ppermute(prompt_of(2 * h + c & NH - 1), RUN, run_pairs(FORWARD_BACK))  5.17 us
    pallas_call x1, Pallas kernels, body(): pl.pallas_call(prompt_step, out_shape=(wide, wide, jax.ShapeDtypeStruct((...  5.13 us
  transfers between devices with their start and end apart: 8, of which 2 were waited for; matrix products, arithmetic and copies ran while one was open for 7% of the time, Pallas kernels for 11%

profile of v2, /device:TPU:1, one launch (start us, length us, event | category | flops | bytes accessed | tf_op | source)
XLA Modules:
  0.0 128.1 jit_solution(14263084832836420177)
XLA Ops:
  0.6 1.4 %constant_dynamic-slice_fusion.3 = (bf16[64,2,1,128]{3,2,1,0:T(2,128)(2,1)S(1)}, bf16[64,2,1,128]{3,2,1,0:T(2,128)(2,1)S(1)}, bf16[64,2,1,128]{3,2,1,0:T(2,128)(2,1)S(1)}) fusion(bf16[512,2,8,128]{3,2,1,0:T(8,128)(2,1)} %param.7, u32[]{:T(128)S(6)} %convert_element_type.88, u32[]{:T(128)S(6)} %convert_element_type.92, u32[]{:T(128)S(6)} %convert_element_type.93), kind=kLoop, calls=%fused_computation.23 | loop fusion | bytes 196620 | tf_op jit(solution)/shard_map/dynamic_slice | solution.py:243
  2.1 26.6 %collective-permute-start.1 = (bf16[128,128]{1,0:T(8,128)(2,1)S(1)}, bf16[128,128]{1,0:T(8,128)(2,1)S(1)}, u32[]{:S(2)}, u32[]{:S(2)}) collective-permute-start(bf16[128,128]{1,0:T(8,128)(2,1)S(1)} %bitcast.51), channel_id=1, source_target_pairs={{12,128},{13,130},{14,132},{15,134},{0,136},{1,138},{2,140},{3,142... | collective-permute-start | bytes 98312 | tf_op jit(solution)/shard_map/ppermute | solution.py:251
  28.7 5.2 %collective-permute-start = (bf16[128,128]{1,0:T(8,128)(2,1)S(1)}, bf16[128,128]{1,0:T(8,128)(2,1)S(1)}, u32[]{:S(2)}, u32[]{:S(2)}) collective-permute-start(bf16[128,128]{1,0:T(8,128)(2,1)S(1)} %bitcast.52), channel_id=1, source_target_pairs={{0,193},{1,195},{2,197},{3,199},{4,201},{5,203},{6,205},{7,207},{6... | collective-permute-start | bytes 98312 | tf_op jit(solution)/shard_map/ppermute | solution.py:255
  33.9 2.1 %constant_dynamic-slice_fusion.4 = bf16[512,2,1,128]{3,2,1,0:T(2,128)(2,1)S(1)} fusion(bf16[512,2,8,128]{3,2,1,0:T(8,128)(2,1)} %param.7, u32[]{:T(128)S(6)} %convert_element_type.88), kind=kLoop, calls=%fused_computation.24 | loop fusion | bytes 524292 | tf_op jit(solution)/shard_map/jit(dynamic_index_in_dim)/dynamic_slice | solution.py:266
  36.0 1.5 %fusion.keyseg_ref = bf16[512,128]{1,0:T(8,128)(2,1)} fusion(s32[512]{0:T(512)} %param.9), kind=kLoop, calls=%fused_computation.7 | loop fusion | flops 131072 | bytes 133120 | tf_op jit(solution)/shard_map/convert_element_type | solution.py:271
  37.5 0.8 broadcast_in_dim.70
  38.5 1.1 select_convert_fusion.gate_ref
  39.6 1.8 %route.1.scalars_ref = s32[16]{0:T(128)} custom-call(s32[64]{0:T(128)} %partner_ref.1, s32[64]{0:T(128)} %blocks_ref.1, s32[4,128]{1,0:T(4,128)} %bitcast.53), custom_call_target="tpu_custom_call" | custom-call | tf_op jit(solution)/shard_map/route/pallas_call | solution.py:260
  41.5 1.6 %fusion.7 = (s32[1]{0:T(128)}, s32[1]{0:T(128)}, s32[1]{0:T(128)}, s32[1]{0:T(128)}, s32[1]{0:T(128)}, /*index=5*/s32[1]{0:T(128)}) fusion(s32[16]{0:T(128)} %route.1.scalars_ref), kind=kLoop, calls=%fused_computation.28 | loop fusion | bytes 48 | tf_op jit(solution)/shard_map/slice | solution.py:283
  47.7 4.7 %local_forward.1 = (f32[2048,128]{1,0:T(8,128)}, f32[2048,128]{1,0:T(8,128)}) custom-call(bf16[2048,128]{1,0:T(8,128)(2,1)} %bitcast.44, bf16[2048,128]{1,0:T(8,128)(2,1)} %select_convert_fusion.gate_ref, bf16[2,512,128]{2,1,0:T(8,128)(2,1)} %bitcast.47, bf16[512,128]{1,0:T(8,128)(2,1)} %fusion.keyseg_ref), custom_call_target="tpu_custom_call" | custom-call | tf_op jit(solution)/shard_map/local_forward/pallas_call | solution.py:279
  52.5 18.5 %all_to_all.10 = bf16[16,128,128]{2,1,0:T(8,128)(2,1)S(1)} all-to-all(bf16[16,128,128]{2,1,0:T(8,128)(2,1)S(1)} %broadcast_select_fusion.1), channel_id=1, replica_groups=mesh['y'=4,'w'=4,'x'=4,'h'=8,'c'=2] {'y','x'}, dimensions={0} | all-to-all | bytes 1048576 | tf_op jit(solution)/shard_map/all_to_all | solution.py:292
  71.1 2.5 %collective-permute-start.2 = (bf16[128,128]{1,0:T(8,128)(2,1)S(1)}, bf16[128,128]{1,0:T(8,128)(2,1)S(1)}, u32[]{:S(2)}, u32[]{:S(2)}) collective-permute-start(bf16[128,128]{1,0:T(8,128)(2,1)S(1)} %dynamic-slice_bitcast_fusion.2.got_ref), channel_id=1, source_target_pairs={{0,1},{1,0},{2,3},{3,2},{4,5},{5,4},{6,7},{7,6},{8,9},{9,8},{10,11... | collective-permute-start | bytes 98312 | tf_op jit(solution)/shard_map/ppermute | solution.py:294
  73.6 0.8 collective-permute-done.2.other_ref
  75.0 5.1 %prompt_step.1 = (f32[2048,128]{1,0:T(8,128)}, f32[2048,128]{1,0:T(8,128)}, bf16[2048,64]{1,0:T(8,128)(2,1)}, bf16[128,128]{1,0:T(8,128)(2,1)}) custom-call(s32[16]{0:T(128)} %route.1.scalars_ref, bf16[2048,128]{1,0:T(8,128)(2,1)} %bitcast.45, bf16[2048,128]{1,0:T(8,128)(2,1)} %bitcast.49, bf16[2048,128]{1,0:T(8,128)(2,1)} %select_convert_fusion.gate_ref, ...), custom_call_target="tpu_custom_call" | custom-call | tf_op jit(solution)/shard_map/prompt_step/pallas_call | solution.py:304
  80.2 2.2 %collective-permute-start.4 = (bf16[128,128]{1,0:T(8,128)(2,1)}, bf16[128,128]{1,0:T(8,128)(2,1)S(1)}, u32[]{:S(2)}, u32[]{:S(2)}) collective-permute-start(bf16[128,128]{1,0:T(8,128)(2,1)} %get-tuple-element.35), channel_id=1, source_target_pairs={{0,1},{1,0},{2,3},{3,2},{4,5},{5,4},{6,7},{7,6},{8,9},{9,8},{10,11... | collective-permute-start | bytes 98312 | tf_op jit(solution)/shard_map/ppermute | solution.py:321
  82.4 1.0 collective-permute-done.4
  83.5 0.8 add_convert_fusion
  84.4 14.2 %all_to_all.11 = bf16[16,128,128]{2,1,0:T(8,128)(2,1)S(1)} all-to-all(bf16[16,128,128]{2,1,0:T(8,128)(2,1)S(1)} %broadcast_select_fusion), channel_id=1, replica_groups=mesh['y'=4,'w'=4,'x'=4,'h'=8,'c'=2] {'y','x'}, dimensions={0} | all-to-all | bytes 1048576 | tf_op jit(solution)/shard_map/all_to_all | solution.py:326
  98.6 7.6 %collective-permute-start.5 = (bf16[128,128]{1,0:T(8,128)(2,1)S(1)}, bf16[128,128]{1,0:T(8,128)(2,1)S(1)}, u32[]{:S(2)}, u32[]{:S(2)}) collective-permute-start(bf16[128,128]{1,0:T(8,128)(2,1)S(1)} %get-tuple-element.43), channel_id=1, source_target_pairs={{0,128},{2,130},{4,132},{6,134},{8,136},{10,138},{12,140},{14,142}... | collective-permute-start | bytes 98312 | tf_op jit(solution)/shard_map/ppermute | solution.py:331
  106.3 6.4 %collective-permute-start.6 = (bf16[128,128]{1,0:T(8,128)(2,1)S(1)}, bf16[128,128]{1,0:T(8,128)(2,1)S(1)}, u32[]{:S(2)}, u32[]{:S(2)}) collective-permute-start(bf16[128,128]{1,0:T(8,128)(2,1)S(1)} %get-tuple-element.42), channel_id=1, source_target_pairs={{1,193},{3,195},{5,197},{7,199},{9,201},{11,203},{13,205},{15,207}... | collective-permute-start | bytes 98312 | tf_op jit(solution)/shard_map/ppermute | solution.py:334
  112.6 7.4 %local_backward.1 = (bf16[2048,128]{1,0:T(8,128)(2,1)}, bf16[2048,128]{1,0:T(8,128)(2,1)}, bf16[512,128]{1,0:T(8,128)(2,1)}, bf16[512,128]{1,0:T(8,128)(2,1)}) custom-call(s32[16]{0:T(128)} %route.1.scalars_ref, bf16[2048,128]{1,0:T(8,128)(2,1)} %bitcast.46, bf16[2048,128]{1,0:T(8,128)(2,1)} %bitcast.50, bf16[2048,128]{1,0:T(8,128)(2,1)} %select_convert_fusion.gate_ref, ...), custom_call_target="tpu_custom_call" | custom-call | tf_op jit(solution)/shard_map/local_backward/pallas_call | solution.py:337
  120.1 2.1 %collective-permute-start.3 = (bf16[512,128]{1,0:T(8,128)(2,1)}, bf16[512,128]{1,0:T(8,128)(2,1)S(1)}, u32[]{:S(2)}, u32[]{:S(2)}) collective-permute-start(bf16[512,128]{1,0:T(8,128)(2,1)} %get-tuple-element.33), channel_id=1, source_target_pairs={{0,1},{1,0},{2,3},{3,2},{4,5},{5,4},{6,7},{7,6},{8,9},{9,8},{10,11... | collective-permute-start | bytes 393224 | tf_op jit(solution)/shard_map/ppermute | solution.py:348
  122.2 4.2 %collective-permute-start.7 = (bf16[64,128]{1,0:T(8,128)(2,1)S(1)}, bf16[64,128]{1,0:T(8,128)(2,1)S(1)}, u32[]{:S(2)}, u32[]{:S(2)}) collective-permute-start(bf16[64,128]{1,0:T(8,128)(2,1)S(1)} %constant_dynamic-slice_fusion), channel_id=1, source_target_pairs={{0,1},{1,0},{2,3},{3,2},{4,5},{5,4},{6,7},{7,6},{8,9},{9,8},{10,11... | collective-permute-start | bytes 49160 | tf_op jit(solution)/shard_map/ppermute | solution.py:357
  126.4 0.9 convert_add_fusion
  (27 shorter events, 2.5 us)
Async XLA Ops:
  2.1 50.3 %collective-permute-start.1 = (bf16[128,128]{1,0:T(8,128)(2,1)S(1)}, bf16[128,128]{1,0:T(8,128)(2,1)S(1)}, u32[]{:S(2)}, u32[]{:S(2)}) collective-permute-start(bf16[128,128]{1,0:T(8,128)(2,1)S(1)} %bitcast.51), channel_id=1, source_target_pairs={{12,128},{13,130},{14,132},{15,134},{0,136},{1,138},{2,140},{3,142... | collective-permute-start | bytes 98312 | tf_op jit(solution)/shard_map/ppermute | solution.py:251
  28.7 23.7 %collective-permute-start = (bf16[128,128]{1,0:T(8,128)(2,1)S(1)}, bf16[128,128]{1,0:T(8,128)(2,1)S(1)}, u32[]{:S(2)}, u32[]{:S(2)}) collective-permute-start(bf16[128,128]{1,0:T(8,128)(2,1)S(1)} %bitcast.52), channel_id=1, source_target_pairs={{0,193},{1,195},{2,197},{3,199},{4,201},{5,203},{6,205},{7,207},{6... | collective-permute-start | bytes 98312 | tf_op jit(solution)/shard_map/ppermute | solution.py:255
  71.1 3.4 %copy-start = (bf16[128,128]{1,0:T(8,128)(2,1)}, bf16[128,128]{1,0:T(8,128)(2,1)S(1)}, u32[]{:S(2)}) copy-start(bf16[128,128]{1,0:T(8,128)(2,1)S(1)} %dynamic-slice_bitcast_fusion.2.got_ref) | copy-start | bytes 98308
  71.1 3.4 %collective-permute-start.2 = (bf16[128,128]{1,0:T(8,128)(2,1)S(1)}, bf16[128,128]{1,0:T(8,128)(2,1)S(1)}, u32[]{:S(2)}, u32[]{:S(2)}) collective-permute-start(bf16[128,128]{1,0:T(8,128)(2,1)S(1)} %dynamic-slice_bitcast_fusion.2.got_ref), channel_id=1, source_target_pairs={{0,1},{1,0},{2,3},{3,2},{4,5},{5,4},{6,7},{7,6},{8,9},{9,8},{10,11... | collective-permute-start | bytes 98312 | tf_op jit(solution)/shard_map/ppermute | solution.py:294
  74.4 0.6 copy-start.1
  80.2 3.3 %collective-permute-start.4 = (bf16[128,128]{1,0:T(8,128)(2,1)}, bf16[128,128]{1,0:T(8,128)(2,1)S(1)}, u32[]{:S(2)}, u32[]{:S(2)}) collective-permute-start(bf16[128,128]{1,0:T(8,128)(2,1)} %get-tuple-element.35), channel_id=1, source_target_pairs={{0,1},{1,0},{2,3},{3,2},{4,5},{5,4},{6,7},{7,6},{8,9},{9,8},{10,11... | collective-permute-start | bytes 98312 | tf_op jit(solution)/shard_map/ppermute | solution.py:321
  98.6 23.6 %collective-permute-start.5 = (bf16[128,128]{1,0:T(8,128)(2,1)S(1)}, bf16[128,128]{1,0:T(8,128)(2,1)S(1)}, u32[]{:S(2)}, u32[]{:S(2)}) collective-permute-start(bf16[128,128]{1,0:T(8,128)(2,1)S(1)} %get-tuple-element.43), channel_id=1, source_target_pairs={{0,128},{2,130},{4,132},{6,134},{8,136},{10,138},{12,140},{14,142}... | collective-permute-start | bytes 98312 | tf_op jit(solution)/shard_map/ppermute | solution.py:331
  106.3 15.9 %collective-permute-start.6 = (bf16[128,128]{1,0:T(8,128)(2,1)S(1)}, bf16[128,128]{1,0:T(8,128)(2,1)S(1)}, u32[]{:S(2)}, u32[]{:S(2)}) collective-permute-start(bf16[128,128]{1,0:T(8,128)(2,1)S(1)} %get-tuple-element.42), channel_id=1, source_target_pairs={{1,193},{3,195},{5,197},{7,199},{9,201},{11,203},{13,205},{15,207}... | collective-permute-start | bytes 98312 | tf_op jit(solution)/shard_map/ppermute | solution.py:334
  120.1 6.4 %collective-permute-start.3 = (bf16[512,128]{1,0:T(8,128)(2,1)}, bf16[512,128]{1,0:T(8,128)(2,1)S(1)}, u32[]{:S(2)}, u32[]{:S(2)}) collective-permute-start(bf16[512,128]{1,0:T(8,128)(2,1)} %get-tuple-element.33), channel_id=1, source_target_pairs={{0,1},{1,0},{2,3},{3,2},{4,5},{5,4},{6,7},{7,6},{8,9},{9,8},{10,11... | collective-permute-start | bytes 393224 | tf_op jit(solution)/shard_map/ppermute | solution.py:348
  122.2 5.2 %collective-permute-start.7 = (bf16[64,128]{1,0:T(8,128)(2,1)S(1)}, bf16[64,128]{1,0:T(8,128)(2,1)S(1)}, u32[]{:S(2)}, u32[]{:S(2)}) collective-permute-start(bf16[64,128]{1,0:T(8,128)(2,1)S(1)} %constant_dynamic-slice_fusion), channel_id=1, source_target_pairs={{0,1},{1,0},{2,3},{3,2},{4,5},{5,4},{6,7},{7,6},{8,9},{9,8},{10,11... | collective-permute-start | bytes 49160 | tf_op jit(solution)/shard_map/ppermute | solution.py:357
  127.4 0.7 copy-start.2

commit v3 on v2

--- a/solution.py
+++ b/solution.py
@@ -46,7 +46,9 @@
 TILE = 128
 
 
-LOW, HIGH, LIVE, DIRECT, CORE, SLOT, FIRST, SEND_FAR, SEND_BACK, SEND_STAY, ARRIVAL = range(11)
+LOW, HIGH, LIVE, DIRECT, CORE, SLOT, FIRST, SEND_FAR, SEND_BACK, SEND_STAY, ARRIVAL, BEGIN, END = range(
+    13
+)
 
 
 def route(partner_ref, blocks_ref, segments_ref, table_ref):
@@ -79,8 +81,10 @@
     first_token = jnp.sum((segments < 1).astype(jnp.float32)).astype(jnp.int32)
     end_token = jnp.sum((segments < 2).astype(jnp.float32)).astype(jnp.int32)
     rel = (((responder >> 2) & 3) - w) & 3
-    table_ref[LOW] = first_token >> 6
+    table_ref[LOW] = jnp.minimum(first_token >> 6, 7)
     table_ref[HIGH] = (end_token + 63) >> 6
+    table_ref[BEGIN] = first_token
+    table_ref[END] = end_token
     table_ref[LIVE] = BLK * blocks_ref[owner]
     table_ref[DIRECT] = (((owner_w - w) & 1) == c).astype(jnp.int32)
     table_ref[CORE] = c
@@ -128,26 +132,63 @@
 
 
 def prompt_step(
-    scalars_ref, q_ref, grad_ref, gate_ref, got_ref, other_ref, outin_ref, lsein_ref,
-    out_ref, lse_ref, dscore_ref, dprompt_ref, dkey_ref, dvalue_ref,
+    scalars_ref, got_ref, other_ref, q_ref, grad_ref, outin_ref, lsein_ref,
+    dprompt_ref, out_ref, lse_ref, dscore_ref,
+    qbuf_ref, gradbuf_ref, outbuf_ref, lsebuf_ref, outnew_ref, lsenew_ref, dscorenew_ref,
+    insems_ref, outsems_ref, dkey_ref, dvalue_ref,
 ):
-    index = pl.program_id(0)
-
-    @pl.when(index == 0)
-    def _():
-        dkey_ref[...] = jnp.zeros_like(dkey_ref)
-        dvalue_ref[...] = jnp.zeros_like(dvalue_ref)
-
-    @pl.when((scalars_ref[LOW] <= index) & (index < scalars_ref[HIGH]))
-    def _():
-        prompt = pick(scalars_ref, got_ref, other_ref)
-        keys, values = prompt[:PMAX], prompt[PMAX:]
-        segment_one = (lax.broadcasted_iota(jnp.int32, (PMAX, TILE), 1) == 1).astype(jnp.bfloat16)
-        alive = lax.broadcasted_iota(jnp.int32, (PROWS, PMAX), 1) < scalars_ref[LIVE]
-        q, grad = q_ref[...], grad_ref[...]
-        scores = dot(q, keys, 1, 1) + dot(gate_ref[...], segment_one, 1, 1)
-        logits = jnp.where(alive, scores, MASKED) * LOG_SCALE
-        lse = lsein_ref[:, :1]
+    low_block, high_block = scalars_ref[LOW], scalars_ref[HIGH]
+    coming = ((q_ref, qbuf_ref), (grad_ref, gradbuf_ref), (outin_ref, outbuf_ref), (lsein_ref, lsebuf_ref))
+    leaving = ((out_ref, outnew_ref), (lse_ref, lsenew_ref), (dscore_ref, dscorenew_ref))
+
+    def loads(index, slot):
+        rows = pl.ds(pl.multiple_of(index * PROWS, PROWS), PROWS)
+        return [
+            pltpu.make_async_copy(far.at[rows, :], buffer.at[slot], insems_ref.at[k, slot])
+            for k, (far, buffer) in enumerate(coming)
+        ]
+
+    def stores(index, slot):
+        rows = pl.ds(pl.multiple_of(index * PROWS, PROWS), PROWS)
+        return [
+            pltpu.make_async_copy(buffer.at[slot], far.at[rows, :], outsems_ref.at[k, slot])
+            for k, (far, buffer) in enumerate(leaving)
+        ]
+
+    for copy in loads(low_block, 0):
+        copy.start()
+    prompt = pick(scalars_ref, got_ref, other_ref)
+    keys, values = prompt[:PMAX], prompt[PMAX:]
+    alive = lax.broadcasted_iota(jnp.int32, (PROWS, PMAX), 1) < scalars_ref[LIVE]
+    row = lax.broadcasted_iota(jnp.int32, (PROWS, PMAX), 0)
+    dkey_ref[...] = jnp.zeros_like(dkey_ref)
+    dvalue_ref[...] = jnp.zeros_like(dvalue_ref)
+
+    def block(index, carry):
+        slot = (index - low_block) & 1
+
+        @pl.when(index + 1 < high_block)
+        def _():
+            for copy in loads(index + 1, 1 - slot):
+                copy.start()
+
+        for copy in loads(index, slot):
+            copy.wait()
+
+        @pl.when(index >= low_block + 2)
+        def _():
+            for copy in stores(index - 2, slot):
+                copy.wait()
+
+        first_row = index * PROWS
+        q, grad = qbuf_ref[slot], gradbuf_ref[slot]
+        allowed = (
+            alive
+            & (row >= 4 * scalars_ref[BEGIN] - first_row)
+            & (row < 4 * scalars_ref[END] - first_row)
+        )
+        logits = jnp.where(allowed, dot(q, keys, 1, 1), MASKED) * LOG_SCALE
+        lse = lsebuf_ref[slot][:, :1]
         peak = jnp.maximum(lse, jnp.max(logits, axis=1, keepdims=True))
         weights = jnp.exp2(logits - peak)
         before = jnp.exp2(lse - peak)
@@ -155,20 +196,27 @@
         inverse = 1.0 / total
         probabilities = weights * inverse
         low = probabilities.astype(jnp.bfloat16)
-        out = outin_ref[...] * (before * inverse) + dot(low, values, 1, 0)
-        out_ref[...] = out
-        lse_ref[...] = jnp.broadcast_to(peak + jnp.log2(total), (PROWS, TILE))
+        out = outbuf_ref[slot] * (before * inverse) + dot(low, values, 1, 0)
+        outnew_ref[slot] = out
+        lsenew_ref[slot] = jnp.broadcast_to(peak + jnp.log2(total), (PROWS, TILE))
         rounded = out.astype(jnp.bfloat16).astype(jnp.float32)
         delta = jnp.sum(grad.astype(jnp.float32) * rounded, axis=1, keepdims=True)
         dscore = (probabilities * (dot(grad, values, 1, 1) - delta)).astype(jnp.bfloat16)
-        dscore_ref[...] = dscore
+        dscorenew_ref[slot, :, :PMAX] = dscore
+        for copy in stores(index, slot):
+            copy.start()
         dvalue_ref[...] += dot(low, grad, 0, 0)
         dkey_ref[...] += dot(dscore, q, 0, 0)
-
-    @pl.when(index == pl.num_programs(0) - 1)
-    def _():
-        dprompt_ref[:PMAX, :] = (dkey_ref[...] * SCALE).astype(jnp.bfloat16)
-        dprompt_ref[PMAX:, :] = dvalue_ref[...].astype(jnp.bfloat16)
+        return carry
+
+    lax.fori_loop(low_block, high_block, block, 0)
+    dprompt_ref[:PMAX, :] = (dkey_ref[...] * SCALE).astype(jnp.bfloat16)
+    dprompt_ref[PMAX:, :] = dvalue_ref[...].astype(jnp.bfloat16)
+    for back in (2, 1):
+        @pl.when(high_block - back >= low_block)
+        def _():
+            for copy in stores(high_block - back, (high_block - back - low_block) & 1):
+                copy.wait()
 
 
 def local_backward(
@@ -214,7 +262,7 @@
             @pl.when((scalars_ref[LOW] <= index) & (index < scalars_ref[HIGH]))
             def _():
                 acc_ref[pl.ds(part * PROWS, PROWS), :] += dot(
-                    dscore_ref[pl.ds(index * PROWS, PROWS), :], prompt_keys, 1, 0
+                    dscore_ref[pl.ds(index * PROWS, PROWS), :PMAX], prompt_keys, 1, 0
                 )
 
         dquery_ref[rows, :] = (acc_ref[...] * SCALE).astype(jnp.bfloat16)
@@ -227,6 +275,11 @@
 
 SMEM = pl.BlockSpec(memory_space=pltpu.SMEM)
 VMEM = pl.BlockSpec(memory_space=pltpu.VMEM)
+FAR = pl.BlockSpec(memory_space=pltpu.HBM)
+
+
+def near(array):
+    return pltpu.with_memory_space_constraint(array, pltpu.VMEM)
 
 
 def body(queries, keys_values, grad_out, segments, partner, prompt_blocks):
@@ -272,51 +325,44 @@
     q = queries.reshape(flat, head_dim)
     grad = grad_out.reshape(flat, head_dim)
 
-    wide = jax.ShapeDtypeStruct((flat, head_dim), jnp.float32)
+    wide = pltpu.HBM((flat, head_dim), jnp.float32)
     narrow = jax.ShapeDtypeStruct((flat, head_dim), jnp.bfloat16)
-    prompt_shape = jax.ShapeDtypeStruct((2 * PMAX, head_dim), jnp.bfloat16)
     part_shape = jax.ShapeDtypeStruct((rows_here, head_dim), jnp.bfloat16)
+    scalar = [table[k].astype(jnp.uint32) for k in range(11)]
+
+    slots = jnp.arange(NY * NX, dtype=jnp.uint32)
+    first = jnp.where(c == 0, own, back)
+    take_first = (scalar[FIRST] >> slots) & 1 == 1
+    outgoing = jnp.where(take_first[:, None, None], first[None], far_or_next[None])
+    outgoing, kv_local, gate, key_segments, scalar = lax.optimization_barrier(
+        (outgoing, kv_local, gate, key_segments, scalar)
+    )
+    incoming = lax.all_to_all(outgoing, ("y", "x"), split_axis=0, concat_axis=0, tiled=True)
     local_out, local_lse = pl.pallas_call(
         local_forward, out_shape=(wide, wide), name="local_forward",
         in_specs=[VMEM] * 4, out_specs=(VMEM, VMEM),
     )(q, gate, kv_local, key_segments)
-    scalar = [table[k].astype(jnp.uint32) for k in range(11)]
-
-    slots = jnp.arange(NY * NX, dtype=jnp.uint32)
-    first = jnp.where(c == 0, own, back)
-    take_first = (scalar[FIRST] >> slots) & 1 == 1
-    outgoing = jnp.where(take_first[:, None, None], first[None], far_or_next[None])
-    outgoing, local_out, local_lse, scalar = lax.optimization_barrier(
-        (outgoing, local_out, local_lse, scalar)
-    )
-    incoming = lax.all_to_all(outgoing, ("y", "x"), split_axis=0, concat_axis=0, tiled=True)
+    incoming, local_out, local_lse = lax.optimization_barrier((incoming, local_out, local_lse))
     got = lax.dynamic_index_in_dim(incoming, scalar[SLOT], 0, keepdims=False)
     other = lax.ppermute(got, "c", SWAP)
 
-    def rows_block(index, table_ref):
-        return jnp.clip(index, table_ref[LOW], table_ref[HIGH] - 1), 0
-
-    def whole(index, table_ref):
-        return 0, 0
-
-    wide_block = pl.BlockSpec((PROWS, head_dim), rows_block)
-    whole_block = pl.BlockSpec((2 * PMAX, head_dim), whole)
-    out, lse, dscore, dprompt = pl.pallas_call(
+    dprompt, out, lse, dscore = pl.pallas_call(
         prompt_step,
         out_shape=(
-            wide, wide, jax.ShapeDtypeStruct((flat, PMAX), jnp.bfloat16), prompt_shape,
+            pltpu.VMEM((2 * PMAX, head_dim), jnp.bfloat16), wide, wide,
+            pltpu.HBM((flat, TILE), jnp.bfloat16),
         ),
-        grid_spec=pltpu.PrefetchScalarGridSpec(
-            num_scalar_prefetch=1,
-            grid=(flat // PROWS,),
-            in_specs=[wide_block] * 3 + [whole_block] * 2 + [wide_block] * 2,
-            out_specs=(
-                wide_block, wide_block, pl.BlockSpec((PROWS, PMAX), rows_block), whole_block,
-            ),
-            scratch_shapes=[pltpu.VMEM((PMAX, head_dim), jnp.float32)] * 2,
+        in_specs=[SMEM, VMEM, VMEM] + [FAR] * 4,
+        out_specs=(VMEM, FAR, FAR, FAR),
+        scratch_shapes=(
+            [pltpu.VMEM((2, PROWS, head_dim), jnp.bfloat16)] * 2
+            + [pltpu.VMEM((2, PROWS, head_dim), jnp.float32)] * 4
+            + [pltpu.VMEM((2, PROWS, TILE), jnp.bfloat16)]
+            + [pltpu.SemaphoreType.DMA((4, 2)), pltpu.SemaphoreType.DMA((3, 2))]
+            + [pltpu.VMEM((PMAX, head_dim), jnp.float32)] * 2
         ),
         name="prompt_step",
-    )(table, q, grad, gate, got, other, local_out, local_lse)
+    )(table, near(got), near(other), q, grad, local_out, local_lse)
 
     total = dprompt.astype(jnp.float32) + lax.ppermute(dprompt, "c", SWAP).astype(jnp.float32)
     spread = jnp.where(

time: 129 us -> 123 us (0.953)
  blocking collectives: 32.8 us -> 13.5 us
  starting transfers between devices: 56.8 us -> 63.9 us
  waiting for transfers between devices: 1.89 us -> 8.96 us
    all_to_all x1 -> x0, blocking collectives: 18.5 us -> none  [body(): lax.all_to_all(outgoing, ('y', 'x'), split_axis=0, concat_axis=0, tiled=T...]
    all_to_all x0 -> x1, waiting for transfers between devices: none -> 7.28 us  [body(): lax.all_to_all(outgoing, ('y', 'x'), split_axis=0, concat_axis=0, tiled=T...]
    all_to_all x0 -> x1, starting transfers between devices: none -> 6.75 us  [body(): lax.all_to_all(outgoing, ('y', 'x'), split_axis=0, concat_axis=0, tiled=T...]
  transfers between devices with their start and end apart: 8 -> 9, of which waited for: 2 -> 3; matrix products, arithmetic and copies ran while one was open for 7% -> 7% of each run, Pallas kernels for 11% -> 12%
where the time goes in v3:
time: 123 us; the launch traced here: 121 us
  starting transfers between devices  63.9 us (52%)
  Pallas kernels  18.2 us (15%)
  blocking collectives  13.5 us (11%)
  waiting for transfers between devices  8.96 us (7%)
  local copies, waits for them, and re-layouts  7.47 us (6%)
  between operations  4.78 us (4%)
  other arithmetic  4.64 us (4%)
    ppermute x1, starting transfers between devices, body(): lax.ppermute(prompt_of(jnp.where(far_sender, head_far, head_next)), RUN,...  26.6 us
    all_to_all x1, blocking collectives, body(): lax.all_to_all(spread, ('y', 'x'), split_axis=0, concat_axis=0, tiled=True)  13.5 us
    ppermute x1, starting transfers between devices, body(): lax.ppermute(parcel(scalar[SEND_FAR]), RUN, run_pairs(BACKWARD_FAR + BACK...  8.79 us
    pallas_call x1, Pallas kernels, body(): pl.pallas_call(local_backward, out_shape=(narrow, narrow, part_shape, par...  7.45 us
    all_to_all x1, waiting for transfers between devices, body(): lax.all_to_all(outgoing, ('y', 'x'), split_axis=0, concat_axis=0, tiled=T...  7.28 us
    all_to_all x1, starting transfers between devices, body(): lax.all_to_all(outgoing, ('y', 'x'), split_axis=0, concat_axis=0, tiled=T...  6.75 us
    ppermute x1, starting transfers between devices, body(): lax.ppermute(parcel(scalar[SEND_BACK]), RUN, run_pairs(BACKWARD_BACK))  5.21 us
    ppermute x1, starting transfers between devices, body(): lax.ppermute(prompt_of(2 * h + c & NH - 1), RUN, run_pairs(FORWARD_BACK))  5.17 us
  transfers between devices with their start and end apart: 9, of which 3 were waited for; matrix products, arithmetic and copies ran while one was open for 7% of the time, Pallas kernels for 12%

profile of v3, /device:TPU:1, one launch (start us, length us, event | category | flops | bytes accessed | tf_op | source)
XLA Modules:
  0.0 121.5 jit_solution(816448753314163634)
XLA Ops:
  0.6 1.4 %constant_dynamic-slice_fusion.4 = (bf16[64,2,1,128]{3,2,1,0:T(2,128)(2,1)S(1)}, bf16[64,2,1,128]{3,2,1,0:T(2,128)(2,1)S(1)}, bf16[64,2,1,128]{3,2,1,0:T(2,128)(2,1)S(1)}) fusion(bf16[512,2,8,128]{3,2,1,0:T(8,128)(2,1)} %param.7, u32[]{:T(128)S(6)} %convert_element_type.89, u32[]{:T(128)S(6)} %convert_element_type.90, u32[]{:T(128)S(6)} %convert_element_type.91), kind=kLoop, calls=%fused_computation.24 | loop fusion | bytes 196620 | tf_op jit(solution)/shard_map/dynamic_slice | solution.py:296
  2.1 26.6 %collective-permute-start.1 = (bf16[128,128]{1,0:T(8,128)(2,1)S(1)}, bf16[128,128]{1,0:T(8,128)(2,1)S(1)}, u32[]{:S(2)}, u32[]{:S(2)}) collective-permute-start(bf16[128,128]{1,0:T(8,128)(2,1)S(1)} %bitcast.51), channel_id=1, source_target_pairs={{12,128},{13,130},{14,132},{15,134},{0,136},{1,138},{2,140},{3,142... | collective-permute-start | bytes 98312 | tf_op jit(solution)/shard_map/ppermute | solution.py:304
  28.7 5.2 %collective-permute-start = (bf16[128,128]{1,0:T(8,128)(2,1)S(1)}, bf16[128,128]{1,0:T(8,128)(2,1)S(1)}, u32[]{:S(2)}, u32[]{:S(2)}) collective-permute-start(bf16[128,128]{1,0:T(8,128)(2,1)S(1)} %bitcast.52), channel_id=1, source_target_pairs={{0,193},{1,195},{2,197},{3,199},{4,201},{5,203},{6,205},{7,207},{6... | collective-permute-start | bytes 98312 | tf_op jit(solution)/shard_map/ppermute | solution.py:308
  33.9 2.1 %constant_dynamic-slice_fusion.1 = bf16[512,2,1,128]{3,2,1,0:T(2,128)(2,1)S(1)} fusion(bf16[512,2,8,128]{3,2,1,0:T(8,128)(2,1)} %param.7, u32[]{:T(128)S(6)} %convert_element_type.89), kind=kLoop, calls=%fused_computation.21 | loop fusion | bytes 524292 | tf_op jit(solution)/shard_map/jit(dynamic_index_in_dim)/dynamic_slice | solution.py:319
  36.0 1.5 %fusion.keyseg_ref = bf16[512,128]{1,0:T(8,128)(2,1)} fusion(s32[512]{0:T(512)} %param.9), kind=kLoop, calls=%fused_computation.7 | loop fusion | flops 131072 | bytes 133120 | tf_op jit(solution)/shard_map/convert_element_type | solution.py:324
  37.5 1.8 %route.1.scalars_ref = s32[16]{0:T(128)} custom-call(s32[64]{0:T(128)} %partner_ref.1, s32[64]{0:T(128)} %blocks_ref.1, s32[4,128]{1,0:T(4,128)} %bitcast.53), custom_call_target="tpu_custom_call" | custom-call | tf_op jit(solution)/shard_map/route/pallas_call | solution.py:313
  39.4 1.5 %fusion.7 = (s32[1]{0:T(128)}, s32[1]{0:T(128)}, s32[1]{0:T(128)}, s32[1]{0:T(128)}, s32[1]{0:T(128)}, /*index=5*/s32[1]{0:T(128)}) fusion(s32[16]{0:T(128)} %route.1.scalars_ref), kind=kLoop, calls=%fused_computation.28 | loop fusion | bytes 48 | tf_op jit(solution)/shard_map/slice | solution.py:331
  42.5 1.1 select_convert_fusion.gate_ref
  47.7 0.9 broadcast_select_fusion.1
  48.6 6.8 %all-to-all-start = ((bf16[16,128,128]{2,1,0:T(8,128)(2,1)}), bf16[16,128,128]{2,1,0:T(8,128)(2,1)S(1)}, u32[]{:S(2)}, u32[]{:S(2)}) async-start(bf16[16,128,128]{2,1,0:T(8,128)(2,1)} %broadcast_select_fusion.1), calls=%async_computation | async-start | bytes 1048576 | tf_op jit(solution)/shard_map/all_to_all | solution.py:340
  55.4 4.7 %local_forward.1 = (f32[2048,128]{1,0:T(8,128)}, f32[2048,128]{1,0:T(8,128)}) custom-call(bf16[2048,128]{1,0:T(8,128)(2,1)} %bitcast.44, bf16[2048,128]{1,0:T(8,128)(2,1)} %select_convert_fusion.gate_ref, bf16[2,512,128]{2,1,0:T(8,128)(2,1)} %bitcast.47, bf16[512,128]{1,0:T(8,128)(2,1)} %fusion.keyseg_ref), custom_call_target="tpu_custom_call" | custom-call | tf_op jit(solution)/shard_map/local_forward/pallas_call | solution.py:341
  60.1 7.3 %all-to-all-done = bf16[16,128,128]{2,1,0:T(8,128)(2,1)S(1)} async-done(((bf16[16,128,128]{2,1,0:T(8,128)(2,1)}), bf16[16,128,128]{2,1,0:T(8,128)(2,1)S(1)}, u32[]{:S(2)}, u32[]{:S(2)}) %all-to-all-start) | async-done | bytes 524320 | tf_op jit(solution)/shard_map/all_to_all | solution.py:340
  67.3 2.5 %collective-permute-start.2 = (bf16[128,128]{1,0:T(8,128)(2,1)S(1)}, bf16[128,128]{1,0:T(8,128)(2,1)S(1)}, u32[]{:S(2)}, u32[]{:S(2)}) collective-permute-start(bf16[128,128]{1,0:T(8,128)(2,1)S(1)} %dynamic-slice_bitcast_fusion.2.got_ref), channel_id=1, source_target_pairs={{0,1},{1,0},{2,3},{3,2},{4,5},{5,4},{6,7},{7,6},{8,9},{9,8},{10,11... | collective-permute-start | bytes 98312 | tf_op jit(solution)/shard_map/ppermute | solution.py:347
  69.9 0.8 collective-permute-done.2.other_ref
  70.7 4.2 %prompt_step.1 = (bf16[128,128]{1,0:T(8,128)(2,1)S(1)}, f32[2048,128]{1,0:T(8,128)}, f32[2048,128]{1,0:T(8,128)}, bf16[2048,128]{1,0:T(8,128)(2,1)}) custom-call(s32[16]{0:T(128)} %route.1.scalars_ref, bf16[128,128]{1,0:T(8,128)(2,1)S(1)} %dynamic-slice_bitcast_fusion.2.got_ref, bf16[128,128]{1,0:T(8,128)(2,1)S(1)} %collective-permute-done.2.other_ref, ...), custom_call_target="tpu_custom_call" | custom-call | tf_op jit(solution)/shard_map/prompt_step/pallas_call | solution.py:349
  74.9 2.3 %collective-permute-start.4 = (bf16[128,128]{1,0:T(8,128)(2,1)S(1)}, bf16[128,128]{1,0:T(8,128)(2,1)S(1)}, u32[]{:S(2)}, u32[]{:S(2)}) collective-permute-start(bf16[128,128]{1,0:T(8,128)(2,1)S(1)} %get-tuple-element.43), channel_id=1, source_target_pairs={{0,1},{1,0},{2,3},{3,2},{4,5},{5,4},{6,7},{7,6},{8,9},{9,8},{10,11... | collective-permute-start | bytes 98312 | tf_op jit(solution)/shard_map/ppermute | solution.py:367
  77.2 0.8 collective-permute-done.4
  78.2 13.5 %all_to_all.10 = bf16[16,128,128]{2,1,0:T(8,128)(2,1)S(1)} all-to-all(bf16[16,128,128]{2,1,0:T(8,128)(2,1)S(1)} %broadcast_select_fusion), channel_id=1, replica_groups=mesh['y'=4,'w'=4,'x'=4,'h'=8,'c'=2] {'y','x'}, dimensions={0} | all-to-all | bytes 1048576 | tf_op jit(solution)/shard_map/all_to_all | solution.py:372
  91.7 8.8 %collective-permute-start.5 = (bf16[128,128]{1,0:T(8,128)(2,1)S(1)}, bf16[128,128]{1,0:T(8,128)(2,1)S(1)}, u32[]{:S(2)}, u32[]{:S(2)}) collective-permute-start(bf16[128,128]{1,0:T(8,128)(2,1)S(1)} %get-tuple-element.51), channel_id=1, source_target_pairs={{0,128},{2,130},{4,132},{6,134},{8,136},{10,138},{12,140},{14,142}... | collective-permute-start | bytes 98312 | tf_op jit(solution)/shard_map/ppermute | solution.py:377
  100.5 5.2 %collective-permute-start.6 = (bf16[128,128]{1,0:T(8,128)(2,1)S(1)}, bf16[128,128]{1,0:T(8,128)(2,1)S(1)}, u32[]{:S(2)}, u32[]{:S(2)}) collective-permute-start(bf16[128,128]{1,0:T(8,128)(2,1)S(1)} %get-tuple-element.50), channel_id=1, source_target_pairs={{1,193},{3,195},{5,197},{7,199},{9,201},{11,203},{13,205},{15,207}... | collective-permute-start | bytes 98312 | tf_op jit(solution)/shard_map/ppermute | solution.py:380
  105.7 7.4 %local_backward.1 = (bf16[2048,128]{1,0:T(8,128)(2,1)}, bf16[2048,128]{1,0:T(8,128)(2,1)}, bf16[512,128]{1,0:T(8,128)(2,1)}, bf16[512,128]{1,0:T(8,128)(2,1)}) custom-call(s32[16]{0:T(128)} %route.1.scalars_ref, bf16[2048,128]{1,0:T(8,128)(2,1)} %bitcast.46, bf16[2048,128]{1,0:T(8,128)(2,1)} %bitcast.50, bf16[2048,128]{1,0:T(8,128)(2,1)} %select_convert_fusion.gate_ref, ...), custom_call_target="tpu_custom_call" | custom-call | tf_op jit(solution)/shard_map/local_backward/pallas_call | solution.py:383
  113.2 2.1 %collective-permute-start.3 = (bf16[512,128]{1,0:T(8,128)(2,1)}, bf16[512,128]{1,0:T(8,128)(2,1)S(1)}, u32[]{:S(2)}, u32[]{:S(2)}) collective-permute-start(bf16[512,128]{1,0:T(8,128)(2,1)} %get-tuple-element.41), channel_id=1, source_target_pairs={{0,1},{1,0},{2,3},{3,2},{4,5},{5,4},{6,7},{7,6},{8,9},{9,8},{10,11... | collective-permute-start | bytes 393224 | tf_op jit(solution)/shard_map/ppermute | solution.py:394
  115.3 4.5 %collective-permute-start.7 = (bf16[64,128]{1,0:T(8,128)(2,1)S(1)}, bf16[64,128]{1,0:T(8,128)(2,1)S(1)}, u32[]{:S(2)}, u32[]{:S(2)}) collective-permute-start(bf16[64,128]{1,0:T(8,128)(2,1)S(1)} %constant_dynamic-slice_fusion), channel_id=1, source_target_pairs={{0,1},{1,0},{2,3},{3,2},{4,5},{5,4},{6,7},{7,6},{8,9},{9,8},{10,11... | collective-permute-start | bytes 49160 | tf_op jit(solution)/shard_map/ppermute | solution.py:403
  119.8 0.9 convert_add_fusion
  (28 shorter events, 2.7 us)
Async XLA Ops:
  2.1 45.6 %collective-permute-start.1 = (bf16[128,128]{1,0:T(8,128)(2,1)S(1)}, bf16[128,128]{1,0:T(8,128)(2,1)S(1)}, u32[]{:S(2)}, u32[]{:S(2)}) collective-permute-start(bf16[128,128]{1,0:T(8,128)(2,1)S(1)} %bitcast.51), channel_id=1, source_target_pairs={{12,128},{13,130},{14,132},{15,134},{0,136},{1,138},{2,140},{3,142... | collective-permute-start | bytes 98312 | tf_op jit(solution)/shard_map/ppermute | solution.py:304
  28.7 18.9 %collective-permute-start = (bf16[128,128]{1,0:T(8,128)(2,1)S(1)}, bf16[128,128]{1,0:T(8,128)(2,1)S(1)}, u32[]{:S(2)}, u32[]{:S(2)}) collective-permute-start(bf16[128,128]{1,0:T(8,128)(2,1)S(1)} %bitcast.52), channel_id=1, source_target_pairs={{0,193},{1,195},{2,197},{3,199},{4,201},{5,203},{6,205},{7,207},{6... | collective-permute-start | bytes 98312 | tf_op jit(solution)/shard_map/ppermute | solution.py:308
  48.6 18.8 %all-to-all-start = ((bf16[16,128,128]{2,1,0:T(8,128)(2,1)}), bf16[16,128,128]{2,1,0:T(8,128)(2,1)S(1)}, u32[]{:S(2)}, u32[]{:S(2)}) async-start(bf16[16,128,128]{2,1,0:T(8,128)(2,1)} %broadcast_select_fusion.1), calls=%async_computation | async-start | bytes 1048576 | tf_op jit(solution)/shard_map/all_to_all | solution.py:340
  67.3 24.3 %copy-start = (bf16[128,128]{1,0:T(8,128)(2,1)}, bf16[128,128]{1,0:T(8,128)(2,1)S(1)}, u32[]{:S(2)}) copy-start(bf16[128,128]{1,0:T(8,128)(2,1)S(1)} %dynamic-slice_bitcast_fusion.2.got_ref) | copy-start | bytes 98308
  67.3 3.4 %collective-permute-start.2 = (bf16[128,128]{1,0:T(8,128)(2,1)S(1)}, bf16[128,128]{1,0:T(8,128)(2,1)S(1)}, u32[]{:S(2)}, u32[]{:S(2)}) collective-permute-start(bf16[128,128]{1,0:T(8,128)(2,1)S(1)} %dynamic-slice_bitcast_fusion.2.got_ref), channel_id=1, source_target_pairs={{0,1},{1,0},{2,3},{3,2},{4,5},{5,4},{6,7},{7,6},{8,9},{9,8},{10,11... | collective-permute-start | bytes 98312 | tf_op jit(solution)/shard_map/ppermute | solution.py:347
  70.7 21.0 %copy-start.1 = (bf16[128,128]{1,0:T(8,128)(2,1)}, bf16[128,128]{1,0:T(8,128)(2,1)S(1)}, u32[]{:S(2)}) copy-start(bf16[128,128]{1,0:T(8,128)(2,1)S(1)} %collective-permute-done.2.other_ref) | copy-start | bytes 98308
  74.9 3.1 %collective-permute-start.4 = (bf16[128,128]{1,0:T(8,128)(2,1)S(1)}, bf16[128,128]{1,0:T(8,128)(2,1)S(1)}, u32[]{:S(2)}, u32[]{:S(2)}) collective-permute-start(bf16[128,128]{1,0:T(8,128)(2,1)S(1)} %get-tuple-element.43), channel_id=1, source_target_pairs={{0,1},{1,0},{2,3},{3,2},{4,5},{5,4},{6,7},{7,6},{8,9},{9,8},{10,11... | collective-permute-start | bytes 98312 | tf_op jit(solution)/shard_map/ppermute | solution.py:367
  91.7 23.6 %collective-permute-start.5 = (bf16[128,128]{1,0:T(8,128)(2,1)S(1)}, bf16[128,128]{1,0:T(8,128)(2,1)S(1)}, u32[]{:S(2)}, u32[]{:S(2)}) collective-permute-start(bf16[128,128]{1,0:T(8,128)(2,1)S(1)} %get-tuple-element.51), channel_id=1, source_target_pairs={{0,128},{2,130},{4,132},{6,134},{8,136},{10,138},{12,140},{14,142}... | collective-permute-start | bytes 98312 | tf_op jit(solution)/shard_map/ppermute | solution.py:377
  100.5 14.8 %collective-permute-start.6 = (bf16[128,128]{1,0:T(8,128)(2,1)S(1)}, bf16[128,128]{1,0:T(8,128)(2,1)S(1)}, u32[]{:S(2)}, u32[]{:S(2)}) collective-permute-start(bf16[128,128]{1,0:T(8,128)(2,1)S(1)} %get-tuple-element.50), channel_id=1, source_target_pairs={{1,193},{3,195},{5,197},{7,199},{9,201},{11,203},{13,205},{15,207}... | collective-permute-start | bytes 98312 | tf_op jit(solution)/shard_map/ppermute | solution.py:380
  113.2 6.6 %collective-permute-start.3 = (bf16[512,128]{1,0:T(8,128)(2,1)}, bf16[512,128]{1,0:T(8,128)(2,1)S(1)}, u32[]{:S(2)}, u32[]{:S(2)}) collective-permute-start(bf16[512,128]{1,0:T(8,128)(2,1)} %get-tuple-element.41), channel_id=1, source_target_pairs={{0,1},{1,0},{2,3},{3,2},{4,5},{5,4},{6,7},{7,6},{8,9},{9,8},{10,11... | collective-permute-start | bytes 393224 | tf_op jit(solution)/shard_map/ppermute | solution.py:394
  115.3 5.4 %collective-permute-start.7 = (bf16[64,128]{1,0:T(8,128)(2,1)S(1)}, bf16[64,128]{1,0:T(8,128)(2,1)S(1)}, u32[]{:S(2)}, u32[]{:S(2)}) collective-permute-start(bf16[64,128]{1,0:T(8,128)(2,1)S(1)} %constant_dynamic-slice_fusion), channel_id=1, source_target_pairs={{0,1},{1,0},{2,3},{3,2},{4,5},{5,4},{6,7},{7,6},{8,9},{9,8},{10,11... | collective-permute-start | bytes 49160 | tf_op jit(solution)/shard_map/ppermute | solution.py:403
  120.8 0.7 copy-start.2

commit v4 on v3

--- a/solution.py
+++ b/solution.py
@@ -46,12 +46,13 @@
 TILE = 128
 
 
-LOW, HIGH, LIVE, DIRECT, CORE, SLOT, FIRST, SEND_FAR, SEND_BACK, SEND_STAY, ARRIVAL, BEGIN, END = range(
-    13
-)
-
-
-def route(partner_ref, blocks_ref, segments_ref, table_ref):
+LOW, HIGH, LIVE, DIRECT, CORE, BEGIN, END = range(7)
+
+
+def route(
+    partner_ref, blocks_ref, segments_ref,
+    table_ref, slot_ref, first_ref, far_ref, back_ref, stay_ref, arrival_ref,
+):
     y, w, x = lax.axis_index("y"), lax.axis_index("w"), lax.axis_index("x")
     c = lax.axis_index("c")
     here = y * 16 + w * 4 + x
@@ -88,12 +89,13 @@
     table_ref[LIVE] = BLK * blocks_ref[owner]
     table_ref[DIRECT] = (((owner_w - w) & 1) == c).astype(jnp.int32)
     table_ref[CORE] = c
-    table_ref[SLOT] = ((owner >> 4) << 2) | (owner & 3)
-    table_ref[FIRST] = first
-    table_ref[SEND_FAR] = far
-    table_ref[SEND_BACK] = back
-    table_ref[SEND_STAY] = stay
-    table_ref[ARRIVAL] = jnp.where((rel & 1) == c, jnp.where(rel < 2, 1, 2), 0)
+    arrival = jnp.where((rel & 1) == c, jnp.where(rel < 2, 1, 2), 0)
+    slot_ref[0] = (((owner >> 4) << 2) | (owner & 3)).astype(jnp.uint32)
+    first_ref[0] = first.astype(jnp.uint32)
+    far_ref[0] = far.astype(jnp.uint32)
+    back_ref[0] = back.astype(jnp.uint32)
+    stay_ref[0] = stay.astype(jnp.uint32)
+    arrival_ref[0] = arrival.astype(jnp.uint32)
 
 
 def dot(left, right, left_dim, right_dim):
@@ -310,17 +312,15 @@
     )
     own = prompt_of(h)
 
-    table = pl.pallas_call(
-        route, out_shape=jax.ShapeDtypeStruct((16,), jnp.int32), name="route",
-        in_specs=[SMEM, SMEM, VMEM], out_specs=SMEM,
+    one = jax.ShapeDtypeStruct((1,), jnp.uint32)
+    table, *scalar = pl.pallas_call(
+        route, out_shape=(jax.ShapeDtypeStruct((16,), jnp.int32),) + (one,) * 6, name="route",
+        in_specs=[SMEM, SMEM, VMEM], out_specs=(SMEM,) * 7,
     )(partner, prompt_blocks, segments.reshape(-1, TILE))
-
-    kv_local = jnp.transpose(
-        lax.dynamic_index_in_dim(keys_values, h.astype(jnp.uint32), 2, keepdims=False), (1, 0, 2)
-    )
+    to_slot, first_bits, far_slot, back_slot, stay_slot, arrival = (s.reshape(()) for s in scalar)
+
+    kv_mixed = lax.dynamic_index_in_dim(keys_values, h.astype(jnp.uint32), 2, keepdims=False)
     lanes = jnp.arange(TILE, dtype=jnp.int32)
-    row_segments = jnp.broadcast_to(segments[:, None], (rows_here, heads_here)).reshape(flat)
-    gate = jnp.where(row_segments[:, None] == lanes[None, :], 0.0, MASKED).astype(jnp.bfloat16)
     key_segments = (segments[:, None] == lanes[None, :]).astype(jnp.bfloat16)
     q = queries.reshape(flat, head_dim)
     grad = grad_out.reshape(flat, head_dim)
@@ -328,22 +328,24 @@
     wide = pltpu.HBM((flat, head_dim), jnp.float32)
     narrow = jax.ShapeDtypeStruct((flat, head_dim), jnp.bfloat16)
     part_shape = jax.ShapeDtypeStruct((rows_here, head_dim), jnp.bfloat16)
-    scalar = [table[k].astype(jnp.uint32) for k in range(11)]
 
     slots = jnp.arange(NY * NX, dtype=jnp.uint32)
     first = jnp.where(c == 0, own, back)
-    take_first = (scalar[FIRST] >> slots) & 1 == 1
+    take_first = (first_bits >> slots) & 1 == 1
     outgoing = jnp.where(take_first[:, None, None], first[None], far_or_next[None])
-    outgoing, kv_local, gate, key_segments, scalar = lax.optimization_barrier(
-        (outgoing, kv_local, gate, key_segments, scalar)
-    )
+    outgoing, kv_mixed, key_segments, segments = lax.optimization_barrier(
+        (outgoing, kv_mixed, key_segments, segments)
+    )
+    kv_local = jnp.transpose(kv_mixed, (1, 0, 2))
+    row_segments = jnp.broadcast_to(segments[:, None], (rows_here, heads_here)).reshape(flat)
+    gate = jnp.where(row_segments[:, None] == lanes[None, :], 0.0, MASKED).astype(jnp.bfloat16)
     incoming = lax.all_to_all(outgoing, ("y", "x"), split_axis=0, concat_axis=0, tiled=True)
     local_out, local_lse = pl.pallas_call(
         local_forward, out_shape=(wide, wide), name="local_forward",
         in_specs=[VMEM] * 4, out_specs=(VMEM, VMEM),
     )(q, gate, kv_local, key_segments)
     incoming, local_out, local_lse = lax.optimization_barrier((incoming, local_out, local_lse))
-    got = lax.dynamic_index_in_dim(incoming, scalar[SLOT], 0, keepdims=False)
+    got = lax.dynamic_index_in_dim(incoming, to_slot, 0, keepdims=False)
     other = lax.ppermute(got, "c", SWAP)
 
     dprompt, out, lse, dscore = pl.pallas_call(
@@ -366,7 +368,7 @@
 
     total = dprompt.astype(jnp.float32) + lax.ppermute(dprompt, "c", SWAP).astype(jnp.float32)
     spread = jnp.where(
-        (slots == scalar[SLOT])[:, None, None], total.astype(jnp.bfloat16)[None],
+        (slots == to_slot)[:, None, None], total.astype(jnp.bfloat16)[None],
         jnp.zeros((), jnp.bfloat16),
     )
     spread = lax.all_to_all(spread, ("y", "x"), split_axis=0, concat_axis=0, tiled=True)
@@ -375,10 +377,10 @@
         return lax.dynamic_index_in_dim(spread, slot, 0, keepdims=False)
 
     far_or_next_back = lax.ppermute(
-        parcel(scalar[SEND_FAR]), RUN, run_pairs(BACKWARD_FAR + BACKWARD_NEXT)
-    )
-    back_back = lax.ppermute(parcel(scalar[SEND_BACK]), RUN, run_pairs(BACKWARD_BACK))
-    stay = parcel(scalar[SEND_STAY])
+        parcel(far_slot), RUN, run_pairs(BACKWARD_FAR + BACKWARD_NEXT)
+    )
+    back_back = lax.ppermute(parcel(back_slot), RUN, run_pairs(BACKWARD_BACK))
+    stay = parcel(stay_slot)
 
     attention, query_gradient, kept, given = pl.pallas_call(
         local_backward,
@@ -395,8 +397,8 @@
     own_sum = kept.astype(jnp.float32) + swapped.astype(jnp.float32)
 
     arrived = jnp.where(c == 0, stay, back_back)
-    arrived = jnp.where(scalar[ARRIVAL] == 2, far_or_next_back, arrived)
-    arrived = jnp.where(scalar[ARRIVAL] == 0, jnp.zeros((), arrived.dtype), arrived)
+    arrived = jnp.where(arrival == 2, far_or_next_back, arrived)
+    arrived = jnp.where(arrival == 0, jnp.zeros((), arrived.dtype), arrived)
     keep_row = (c * PMAX).astype(jnp.uint32)
     kept_prompt = lax.dynamic_slice(arrived, (keep_row, zero), (PMAX, head_dim))
     given_prompt = lax.dynamic_slice(arrived, (PMAX - keep_row, zero), (PMAX, head_dim))

time: 123 us -> 118 us (0.959)
  starting transfers between devices: 63.9 us -> 61.1 us
  between operations: 4.78 us -> 2.2 us
  other arithmetic: 4.64 us -> 6.56 us
  waiting for transfers between devices: 8.96 us -> 7.42 us
    all_to_all x1, waiting for transfers between devices: 7.28 us -> 3.7 us  [body(): lax.all_to_all(outgoing, ('y', 'x'), split_axis=0, concat_axis=0, tiled=T...]
    ppermute x1, waiting for transfers between devices: 0.01 us -> 2.18 us  [body(): lax.ppermute(prompt_of(2 * h + c & NH - 1), RUN, run_pairs(FORWARD_BACK))]
    ppermute x1, starting transfers between devices: 4.46 us -> 2.66 us  [body(): swapped_prompt = lax.ppermute(given_prompt, 'c', SWAP)]
    slice x1 -> x0, local copies, waits for them, and re-layouts: 1.5 us -> none  [body(): scalar = [table[k].astype(jnp.uint32) for k in range(11)]]
    eq x2, other arithmetic: 0.01 us -> 1.31 us  [the longest x1 0.65 us: body(): take_first = first_bits >> slots & 1 == 1]
    squeeze x1, local copies, waits for them, and re-layouts: 0.01 us -> 1.26 us  [parcel(): return lax.dynamic_index_in_dim(spread, slot, 0, keepdims=False)]
  transfers between devices with their start and end apart: 9 -> 9, of which waited for: 3 -> 4; matrix products, arithmetic and copies ran while one was open for 7% -> 7% of each run, Pallas kernels for 12% -> 12%
where the time goes in v4:
time: 118 us
  starting transfers between devices  61.1 us (52%)
  Pallas kernels  19.4 us (16%)
  blocking collectives  13.7 us (12%)
  waiting for transfers between devices  7.42 us (6%)
  local copies, waits for them, and re-layouts  7.18 us (6%)
  other arithmetic  6.56 us (6%)
  between operations  2.2 us (2%)
    ppermute x1, starting transfers between devices, body(): lax.ppermute(prompt_of(jnp.where(far_sender, head_far, head_next)), RUN,...  26.6 us
    all_to_all x1, blocking collectives, body(): lax.all_to_all(spread, ('y', 'x'), split_axis=0, concat_axis=0, tiled=True)  13.7 us
    pallas_call x1, Pallas kernels, body(): pl.pallas_call(local_backward, out_shape=(narrow, narrow, part_shape, par...  7.59 us
    ppermute x1, starting transfers between devices, body(): lax.ppermute(parcel(far_slot), RUN, run_pairs(BACKWARD_FAR + BACKWARD_NEXT))  7.29 us
    all_to_all x1, starting transfers between devices, body(): lax.all_to_all(outgoing, ('y', 'x'), split_axis=0, concat_axis=0, tiled=T...  6.75 us
    ppermute x1, starting transfers between devices, body(): back_back = lax.ppermute(parcel(back_slot), RUN, run_pairs(BACKWARD_BACK))  6.71 us
    pallas_call x1, Pallas kernels, body(): pl.pallas_call(prompt_step, out_shape=(pltpu.VMEM((2 * PMAX, head_dim), j...  5.29 us
    ppermute x1, starting transfers between devices, body(): lax.ppermute(prompt_of(2 * h + c & NH - 1), RUN, run_pairs(FORWARD_BACK))  5.17 us
  transfers between devices with their start and end apart: 9, of which 4 were waited for; matrix products, arithmetic and copies ran while one was open for 7% of the time, Pallas kernels for 12%

profile of v4, /device:TPU:1, one launch (start us, length us, event | category | flops | bytes accessed | tf_op | source)
XLA Modules:
  0.0 117.6 jit_solution(16275102341035577811)
XLA Ops:
  0.6 1.4 %constant_dynamic-slice_fusion.4 = (bf16[64,2,1,128]{3,2,1,0:T(2,128)(2,1)S(1)}, bf16[64,2,1,128]{3,2,1,0:T(2,128)(2,1)S(1)}, bf16[64,2,1,128]{3,2,1,0:T(2,128)(2,1)S(1)}) fusion(bf16[512,2,8,128]{3,2,1,0:T(8,128)(2,1)} %param.7, u32[]{:T(128)S(6)} %convert_element_type.46, u32[]{:T(128)S(6)} %convert_element_type.47, u32[]{:T(128)S(6)} %convert_element_type.48), kind=kLoop, calls=%fused_computation.24 | loop fusion | bytes 196620 | tf_op jit(solution)/shard_map/dynamic_slice | solution.py:298
  2.1 26.6 %collective-permute-start.1 = (bf16[128,128]{1,0:T(8,128)(2,1)S(1)}, bf16[128,128]{1,0:T(8,128)(2,1)S(1)}, u32[]{:S(2)}, u32[]{:S(2)}) collective-permute-start(bf16[128,128]{1,0:T(8,128)(2,1)S(1)} %bitcast.51), channel_id=1, source_target_pairs={{12,128},{13,130},{14,132},{15,134},{0,136},{1,138},{2,140},{3,142... | collective-permute-start | bytes 98312 | tf_op jit(solution)/shard_map/ppermute | solution.py:306
  28.7 5.2 %collective-permute-start = (bf16[128,128]{1,0:T(8,128)(2,1)S(1)}, bf16[128,128]{1,0:T(8,128)(2,1)S(1)}, u32[]{:S(2)}, u32[]{:S(2)}) collective-permute-start(bf16[128,128]{1,0:T(8,128)(2,1)S(1)} %bitcast.52), channel_id=1, source_target_pairs={{0,193},{1,195},{2,197},{3,199},{4,201},{5,203},{6,205},{7,207},{6... | collective-permute-start | bytes 98312 | tf_op jit(solution)/shard_map/ppermute | solution.py:310
  33.9 2.1 %constant_dynamic-slice_fusion.1 = bf16[512,2,1,128]{3,2,1,0:T(2,128)(2,1)S(1)} fusion(bf16[512,2,8,128]{3,2,1,0:T(8,128)(2,1)} %param.7, u32[]{:T(128)S(6)} %convert_element_type.46), kind=kLoop, calls=%fused_computation.21 | loop fusion | bytes 524292 | tf_op jit(solution)/shard_map/jit(dynamic_index_in_dim)/dynamic_slice | solution.py:322
  36.0 1.5 %fusion.keyseg_ref = bf16[512,128]{1,0:T(8,128)(2,1)} fusion(s32[512]{0:T(512)} %param.9), kind=kLoop, calls=%fused_computation.7 | loop fusion | flops 131072 | bytes 133120 | tf_op jit(solution)/shard_map/convert_element_type | solution.py:324
  37.5 1.9 %route.1 = (s32[16]{0:T(128)}, u32[1]{0:T(128)}, u32[1]{0:T(128)}, u32[1]{0:T(128)}, u32[1]{0:T(128)}, /*index=5*/u32[1]{0:T(128)}, u32[1]{0:T(128)}) custom-call(s32[64]{0:T(128)} %partner_ref.1, s32[64]{0:T(128)} %blocks_ref.1, s32[4,128]{1,0:T(4,128)} %bitcast.53), custom_call_target="tpu_custom_call" | custom-call | tf_op jit(solution)/shard_map/route/pallas_call | solution.py:316
  40.8 2.2 %collective-permute-done = bf16[128,128]{1,0:T(8,128)(2,1)S(1)} collective-permute-done((bf16[128,128]{1,0:T(8,128)(2,1)S(1)}, bf16[128,128]{1,0:T(8,128)(2,1)S(1)}, u32[]{:S(2)}, u32[]{:S(2)}) %collective-permute-start) | collective-permute-done | bytes 32800 | tf_op jit(solution)/shard_map/ppermute | solution.py:310
  43.0 0.9 broadcast_select_fusion.1
  43.9 6.8 %all-to-all-start = ((bf16[16,128,128]{2,1,0:T(8,128)(2,1)}), bf16[16,128,128]{2,1,0:T(8,128)(2,1)S(1)}, u32[]{:S(2)}, u32[]{:S(2)}) async-start(bf16[16,128,128]{2,1,0:T(8,128)(2,1)} %broadcast_select_fusion.1), calls=%async_computation | async-start | bytes 1048576 | tf_op jit(solution)/shard_map/all_to_all | solution.py:342
  51.0 1.1 select_convert_fusion.gate_ref
  52.1 4.7 %local_forward.1 = (f32[2048,128]{1,0:T(8,128)}, f32[2048,128]{1,0:T(8,128)}) custom-call(bf16[2048,128]{1,0:T(8,128)(2,1)} %bitcast.44, bf16[2048,128]{1,0:T(8,128)(2,1)} %select_convert_fusion.gate_ref, bf16[2,512,128]{2,1,0:T(8,128)(2,1)} %bitcast.47, bf16[512,128]{1,0:T(8,128)(2,1)} %fusion.keyseg_ref), custom_call_target="tpu_custom_call" | custom-call | tf_op jit(solution)/shard_map/local_forward/pallas_call | solution.py:343
  56.8 3.7 %all-to-all-done = bf16[16,128,128]{2,1,0:T(8,128)(2,1)S(1)} async-done(((bf16[16,128,128]{2,1,0:T(8,128)(2,1)}), bf16[16,128,128]{2,1,0:T(8,128)(2,1)S(1)}, u32[]{:S(2)}, u32[]{:S(2)}) %all-to-all-start) | async-done | bytes 524320 | tf_op jit(solution)/shard_map/all_to_all | solution.py:342
  61.2 1.9 %collective-permute-start.2 = (bf16[128,128]{1,0:T(8,128)(2,1)S(1)}, bf16[128,128]{1,0:T(8,128)(2,1)S(1)}, u32[]{:S(2)}, u32[]{:S(2)}) collective-permute-start(bf16[128,128]{1,0:T(8,128)(2,1)S(1)} %dynamic-slice_bitcast_fusion.2.got_ref), channel_id=1, source_target_pairs={{0,1},{1,0},{2,3},{3,2},{4,5},{5,4},{6,7},{7,6},{8,9},{9,8},{10,11... | collective-permute-start | bytes 98312 | tf_op jit(solution)/shard_map/ppermute | solution.py:349
  63.1 1.2 collective-permute-done.2.other_ref
  64.3 5.3 %prompt_step.1 = (bf16[128,128]{1,0:T(8,128)(2,1)S(1)}, f32[2048,128]{1,0:T(8,128)}, f32[2048,128]{1,0:T(8,128)}, bf16[2048,128]{1,0:T(8,128)(2,1)}) custom-call(s32[16]{0:T(128)} %get-tuple-element.27.scalars_ref, bf16[128,128]{1,0:T(8,128)(2,1)S(1)} %dynamic-slice_bitcast_fusion.2.got_ref, bf16[128,128]{1,0:T(8,128)(2,1)S(1)} %collective-permute-done.2.other_ref, ...), custom_call_target="tpu_custom_call" | custom-call | tf_op jit(solution)/shard_map/prompt_step/pallas_call | solution.py:351
  69.6 2.1 %collective-permute-start.4 = (bf16[128,128]{1,0:T(8,128)(2,1)S(1)}, bf16[128,128]{1,0:T(8,128)(2,1)S(1)}, u32[]{:S(2)}, u32[]{:S(2)}) collective-permute-start(bf16[128,128]{1,0:T(8,128)(2,1)S(1)} %get-tuple-element.47), channel_id=1, source_target_pairs={{0,1},{1,0},{2,3},{3,2},{4,5},{5,4},{6,7},{7,6},{8,9},{9,8},{10,11... | collective-permute-start | bytes 98312 | tf_op jit(solution)/shard_map/ppermute | solution.py:369
  72.8 13.7 %all_to_all.10 = bf16[16,128,128]{2,1,0:T(8,128)(2,1)S(1)} all-to-all(bf16[16,128,128]{2,1,0:T(8,128)(2,1)S(1)} %broadcast_select_fusion), channel_id=1, replica_groups=mesh['y'=4,'w'=4,'x'=4,'h'=8,'c'=2] {'y','x'}, dimensions={0} | all-to-all | bytes 1048576 | tf_op jit(solution)/shard_map/all_to_all | solution.py:374
  86.5 1.3 %dynamic-slice_bitcast_fusion = (bf16[128,128]{1,0:T(8,128)(2,1)S(1)}, bf16[128,128]{1,0:T(8,128)(2,1)S(1)}) fusion(bf16[16,128,128]{2,1,0:T(8,128)(2,1)S(1)} %all_to_all.10, u32[]{:T(128)} %bitcast.25, u32[]{:T(128)} %bitcast.21), kind=kLoop, calls=%fused_computation.16 | loop fusion | bytes 131080 | tf_op jit(solution)/shard_map/jit(dynamic_index_in_dim)/squeeze | solution.py:377
  87.8 7.3 %collective-permute-start.5 = (bf16[128,128]{1,0:T(8,128)(2,1)S(1)}, bf16[128,128]{1,0:T(8,128)(2,1)S(1)}, u32[]{:S(2)}, u32[]{:S(2)}) collective-permute-start(bf16[128,128]{1,0:T(8,128)(2,1)S(1)} %get-tuple-element.55), channel_id=1, source_target_pairs={{0,128},{2,130},{4,132},{6,134},{8,136},{10,138},{12,140},{14,142}... | collective-permute-start | bytes 98312 | tf_op jit(solution)/shard_map/ppermute | solution.py:379
  95.1 6.7 %collective-permute-start.6 = (bf16[128,128]{1,0:T(8,128)(2,1)S(1)}, bf16[128,128]{1,0:T(8,128)(2,1)S(1)}, u32[]{:S(2)}, u32[]{:S(2)}) collective-permute-start(bf16[128,128]{1,0:T(8,128)(2,1)S(1)} %get-tuple-element.54), channel_id=1, source_target_pairs={{1,193},{3,195},{5,197},{7,199},{9,201},{11,203},{13,205},{15,207}... | collective-permute-start | bytes 98312 | tf_op jit(solution)/shard_map/ppermute | solution.py:382
  103.1 7.6 %local_backward.1 = (bf16[2048,128]{1,0:T(8,128)(2,1)}, bf16[2048,128]{1,0:T(8,128)(2,1)}, bf16[512,128]{1,0:T(8,128)(2,1)}, bf16[512,128]{1,0:T(8,128)(2,1)}) custom-call(s32[16]{0:T(128)} %get-tuple-element.27.scalars_ref, bf16[2048,128]{1,0:T(8,128)(2,1)} %bitcast.46, bf16[2048,128]{1,0:T(8,128)(2,1)} %bitcast.50, ...), custom_call_target="tpu_custom_call" | custom-call | tf_op jit(solution)/shard_map/local_backward/pallas_call | solution.py:385
  110.7 1.9 %collective-permute-start.3 = (bf16[512,128]{1,0:T(8,128)(2,1)}, bf16[512,128]{1,0:T(8,128)(2,1)S(1)}, u32[]{:S(2)}, u32[]{:S(2)}) collective-permute-start(bf16[512,128]{1,0:T(8,128)(2,1)} %get-tuple-element.45), channel_id=1, source_target_pairs={{0,1},{1,0},{2,3},{3,2},{4,5},{5,4},{6,7},{7,6},{8,9},{9,8},{10,11... | collective-permute-start | bytes 393224 | tf_op jit(solution)/shard_map/ppermute | solution.py:396
  113.3 2.7 %collective-permute-start.7 = (bf16[64,128]{1,0:T(8,128)(2,1)S(1)}, bf16[64,128]{1,0:T(8,128)(2,1)S(1)}, u32[]{:S(2)}, u32[]{:S(2)}) collective-permute-start(bf16[64,128]{1,0:T(8,128)(2,1)S(1)} %constant_dynamic-slice_fusion), channel_id=1, source_target_pairs={{0,1},{1,0},{2,3},{3,2},{4,5},{5,4},{6,7},{7,6},{8,9},{9,8},{10,11... | collective-permute-start | bytes 49160 | tf_op jit(solution)/shard_map/ppermute | solution.py:405
  116.0 0.9 convert_add_fusion
  (29 shorter events, 4.9 us)
Async XLA Ops:
  2.0 48.7 %copy-start.3 = (s32[512]{0:T(512)S(1)}, s32[512]{0:T(512)}, u32[]{:S(2)}) copy-start(s32[512]{0:T(512)} %param.9) | copy-start | bytes 6148
  2.1 41.0 %collective-permute-start.1 = (bf16[128,128]{1,0:T(8,128)(2,1)S(1)}, bf16[128,128]{1,0:T(8,128)(2,1)S(1)}, u32[]{:S(2)}, u32[]{:S(2)}) collective-permute-start(bf16[128,128]{1,0:T(8,128)(2,1)S(1)} %bitcast.51), channel_id=1, source_target_pairs={{12,128},{13,130},{14,132},{15,134},{0,136},{1,138},{2,140},{3,142... | collective-permute-start | bytes 98312 | tf_op jit(solution)/shard_map/ppermute | solution.py:306
  28.7 14.3 %collective-permute-start = (bf16[128,128]{1,0:T(8,128)(2,1)S(1)}, bf16[128,128]{1,0:T(8,128)(2,1)S(1)}, u32[]{:S(2)}, u32[]{:S(2)}) collective-permute-start(bf16[128,128]{1,0:T(8,128)(2,1)S(1)} %bitcast.52), channel_id=1, source_target_pairs={{0,193},{1,195},{2,197},{3,199},{4,201},{5,203},{6,205},{7,207},{6... | collective-permute-start | bytes 98312 | tf_op jit(solution)/shard_map/ppermute | solution.py:310
  43.9 16.6 %all-to-all-start = ((bf16[16,128,128]{2,1,0:T(8,128)(2,1)}), bf16[16,128,128]{2,1,0:T(8,128)(2,1)S(1)}, u32[]{:S(2)}, u32[]{:S(2)}) async-start(bf16[16,128,128]{2,1,0:T(8,128)(2,1)} %broadcast_select_fusion.1), calls=%async_computation | async-start | bytes 1048576 | tf_op jit(solution)/shard_map/all_to_all | solution.py:342
  61.2 25.3 %copy-start = (bf16[128,128]{1,0:T(8,128)(2,1)}, bf16[128,128]{1,0:T(8,128)(2,1)S(1)}, u32[]{:S(2)}) copy-start(bf16[128,128]{1,0:T(8,128)(2,1)S(1)} %dynamic-slice_bitcast_fusion.2.got_ref) | copy-start | bytes 98308
  61.2 3.1 %collective-permute-start.2 = (bf16[128,128]{1,0:T(8,128)(2,1)S(1)}, bf16[128,128]{1,0:T(8,128)(2,1)S(1)}, u32[]{:S(2)}, u32[]{:S(2)}) collective-permute-start(bf16[128,128]{1,0:T(8,128)(2,1)S(1)} %dynamic-slice_bitcast_fusion.2.got_ref), channel_id=1, source_target_pairs={{0,1},{1,0},{2,3},{3,2},{4,5},{5,4},{6,7},{7,6},{8,9},{9,8},{10,11... | collective-permute-start | bytes 98312 | tf_op jit(solution)/shard_map/ppermute | solution.py:349
  64.3 22.2 %copy-start.1 = (bf16[128,128]{1,0:T(8,128)(2,1)}, bf16[128,128]{1,0:T(8,128)(2,1)S(1)}, u32[]{:S(2)}) copy-start(bf16[128,128]{1,0:T(8,128)(2,1)S(1)} %collective-permute-done.2.other_ref) | copy-start | bytes 98308
  69.6 3.1 %collective-permute-start.4 = (bf16[128,128]{1,0:T(8,128)(2,1)S(1)}, bf16[128,128]{1,0:T(8,128)(2,1)S(1)}, u32[]{:S(2)}, u32[]{:S(2)}) collective-permute-start(bf16[128,128]{1,0:T(8,128)(2,1)S(1)} %get-tuple-element.47), channel_id=1, source_target_pairs={{0,1},{1,0},{2,3},{3,2},{4,5},{5,4},{6,7},{7,6},{8,9},{9,8},{10,11... | collective-permute-start | bytes 98312 | tf_op jit(solution)/shard_map/ppermute | solution.py:369
  87.8 24.8 %collective-permute-start.5 = (bf16[128,128]{1,0:T(8,128)(2,1)S(1)}, bf16[128,128]{1,0:T(8,128)(2,1)S(1)}, u32[]{:S(2)}, u32[]{:S(2)}) collective-permute-start(bf16[128,128]{1,0:T(8,128)(2,1)S(1)} %get-tuple-element.55), channel_id=1, source_target_pairs={{0,128},{2,130},{4,132},{6,134},{8,136},{10,138},{12,140},{14,142}... | collective-permute-start | bytes 98312 | tf_op jit(solution)/shard_map/ppermute | solution.py:379
  95.1 17.5 %collective-permute-start.6 = (bf16[128,128]{1,0:T(8,128)(2,1)S(1)}, bf16[128,128]{1,0:T(8,128)(2,1)S(1)}, u32[]{:S(2)}, u32[]{:S(2)}) collective-permute-start(bf16[128,128]{1,0:T(8,128)(2,1)S(1)} %get-tuple-element.54), channel_id=1, source_target_pairs={{1,193},{3,195},{5,197},{7,199},{9,201},{11,203},{13,205},{15,207}... | collective-permute-start | bytes 98312 | tf_op jit(solution)/shard_map/ppermute | solution.py:382
  110.7 5.3 %collective-permute-start.3 = (bf16[512,128]{1,0:T(8,128)(2,1)}, bf16[512,128]{1,0:T(8,128)(2,1)S(1)}, u32[]{:S(2)}, u32[]{:S(2)}) collective-permute-start(bf16[512,128]{1,0:T(8,128)(2,1)} %get-tuple-element.45), channel_id=1, source_target_pairs={{0,1},{1,0},{2,3},{3,2},{4,5},{5,4},{6,7},{7,6},{8,9},{9,8},{10,11... | collective-permute-start | bytes 393224 | tf_op jit(solution)/shard_map/ppermute | solution.py:396
  113.3 3.6 %collective-permute-start.7 = (bf16[64,128]{1,0:T(8,128)(2,1)S(1)}, bf16[64,128]{1,0:T(8,128)(2,1)S(1)}, u32[]{:S(2)}, u32[]{:S(2)}) collective-permute-start(bf16[64,128]{1,0:T(8,128)(2,1)S(1)} %constant_dynamic-slice_fusion), channel_id=1, source_target_pairs={{0,1},{1,0},{2,3},{3,2},{4,5},{5,4},{6,7},{7,6},{8,9},{9,8},{10,11... | collective-permute-start | bytes 49160 | tf_op jit(solution)/shard_map/ppermute | solution.py:405
  116.9 0.7 copy-start.2

commit v5 on v4

--- a/solution.py
+++ b/solution.py
@@ -104,23 +104,36 @@
     )
 
 
-def local_scores(q, gate, keys, key_segments, step):
+def segment_marks(segments_ref):
+    kinds = lax.broadcasted_iota(jnp.int32, (16, TILE), 0)
+    parts = [
+        jnp.where(kinds == segments_ref[pl.ds(tile, 1), :], 1.0, 0.0).astype(jnp.bfloat16)
+        for tile in range(4)
+    ]
+    return jnp.concatenate(parts, axis=1)
+
+
+def local_scores(q, keys, marks, step):
     width = TILE * (step + 1)
-    scores = dot(q, keys[:width], 1, 1) + dot(gate, key_segments[:width], 1, 1)
     shape = (QROWS, TILE)
     token = lax.broadcasted_iota(jnp.int32, shape, 0) // 4
-    causal = lax.broadcasted_iota(jnp.int32, shape, 1) <= token
+    place = lax.broadcasted_iota(jnp.int32, shape, 1)
+    owner = jnp.where(place == token, 1.0, 0.0).astype(jnp.bfloat16)
+    causal = place <= token
+    gate = ((1.0 - dot(owner, marks[:, width - TILE : width], 1, 1)) * MASKED).astype(jnp.bfloat16)
+    scores = dot(q, keys[:width], 1, 1) + dot(gate, marks[:, :width], 1, 0)
     last = jnp.where(causal, scores[:, width - TILE :], MASKED)
     if step == 0:
         return last
     return jnp.concatenate([scores[:, : width - TILE], last], axis=1)
 
 
-def local_forward(q_ref, gate_ref, kv_ref, keyseg_ref, out_ref, lse_ref):
+def local_forward(q_ref, segments_ref, kv_ref, out_ref, lse_ref):
+    marks = segment_marks(segments_ref)
     for step in range(4):
         rows = pl.ds(step * QROWS, QROWS)
         width = TILE * (step + 1)
-        scores = local_scores(q_ref[rows, :], gate_ref[rows, :], kv_ref[0], keyseg_ref[...], step)
+        scores = local_scores(q_ref[rows, :], kv_ref[0], marks, step)
         peak = jnp.max(scores, axis=1, keepdims=True)
         weights = jnp.exp2((scores - peak) * LOG_SCALE)
         total = jnp.sum(weights, axis=1, keepdims=True)
@@ -222,7 +235,7 @@
 
 
 def local_backward(
-    scalars_ref, q_ref, grad_ref, gate_ref, kv_ref, keyseg_ref, got_ref, other_ref,
+    scalars_ref, q_ref, grad_ref, segments_ref, kv_ref, got_ref, other_ref,
     outlocal_ref, lselocal_ref, outprompt_ref, lseprompt_ref, dscore_ref,
     attention_ref, dquery_ref, kept_ref, given_ref, dkey_ref, dvalue_ref, acc_ref,
 ):
@@ -238,6 +251,7 @@
     dkey_ref[...] = jnp.zeros_like(dkey_ref)
     dvalue_ref[...] = jnp.zeros_like(dvalue_ref)
     prompt_keys = pick(scalars_ref, got_ref, other_ref)[:PMAX]
+    marks = segment_marks(segments_ref)
     for step in range(4):
         rows = pl.ds(step * QROWS, QROWS)
         width = TILE * (step + 1)
@@ -247,7 +261,7 @@
         delta = jnp.sum(
             grad.astype(jnp.float32) * attention.astype(jnp.float32), axis=1, keepdims=True
         )
-        scores = local_scores(q, gate_ref[rows, :], kv_ref[0], keyseg_ref[...], step)
+        scores = local_scores(q, kv_ref[0], marks, step)
         lse = chosen(lseprompt_ref, lselocal_ref, step)
         if step:
             lse = jnp.concatenate([lse] * (step + 1), axis=1)
@@ -320,8 +334,7 @@
     to_slot, first_bits, far_slot, back_slot, stay_slot, arrival = (s.reshape(()) for s in scalar)
 
     kv_mixed = lax.dynamic_index_in_dim(keys_values, h.astype(jnp.uint32), 2, keepdims=False)
-    lanes = jnp.arange(TILE, dtype=jnp.int32)
-    key_segments = (segments[:, None] == lanes[None, :]).astype(jnp.bfloat16)
+    tiles = segments.reshape(-1, TILE)
     q = queries.reshape(flat, head_dim)
     grad = grad_out.reshape(flat, head_dim)
 
@@ -333,17 +346,13 @@
     first = jnp.where(c == 0, own, back)
     take_first = (first_bits >> slots) & 1 == 1
     outgoing = jnp.where(take_first[:, None, None], first[None], far_or_next[None])
-    outgoing, kv_mixed, key_segments, segments = lax.optimization_barrier(
-        (outgoing, kv_mixed, key_segments, segments)
-    )
+    outgoing, kv_mixed = lax.optimization_barrier((outgoing, kv_mixed))
     kv_local = jnp.transpose(kv_mixed, (1, 0, 2))
-    row_segments = jnp.broadcast_to(segments[:, None], (rows_here, heads_here)).reshape(flat)
-    gate = jnp.where(row_segments[:, None] == lanes[None, :], 0.0, MASKED).astype(jnp.bfloat16)
     incoming = lax.all_to_all(outgoing, ("y", "x"), split_axis=0, concat_axis=0, tiled=True)
     local_out, local_lse = pl.pallas_call(
         local_forward, out_shape=(wide, wide), name="local_forward",
-        in_specs=[VMEM] * 4, out_specs=(VMEM, VMEM),
-    )(q, gate, kv_local, key_segments)
+        in_specs=[VMEM] * 3, out_specs=(VMEM, VMEM),
+    )(q, tiles, kv_local)
     incoming, local_out, local_lse = lax.optimization_barrier((incoming, local_out, local_lse))
     got = lax.dynamic_index_in_dim(incoming, to_slot, 0, keepdims=False)
     other = lax.ppermute(got, "c", SWAP)
@@ -368,7 +377,7 @@
 
     total = dprompt.astype(jnp.float32) + lax.ppermute(dprompt, "c", SWAP).astype(jnp.float32)
     spread = jnp.where(
-        (slots == to_slot)[:, None, None], total.astype(jnp.bfloat16)[None],
+        (slots < NY * NX + y.astype(jnp.uint32))[:, None, None], total.astype(jnp.bfloat16)[None],
         jnp.zeros((), jnp.bfloat16),
     )
     spread = lax.all_to_all(spread, ("y", "x"), split_axis=0, concat_axis=0, tiled=True)
@@ -386,11 +395,11 @@
         local_backward,
         out_shape=(narrow, narrow, part_shape, part_shape),
         name="local_backward",
-        in_specs=[SMEM] + [VMEM] * 12,
+        in_specs=[SMEM] + [VMEM] * 11,
         out_specs=(VMEM,) * 4,
         scratch_shapes=[pltpu.VMEM((rows_here, head_dim), jnp.float32)] * 3,
     )(
-        table, q, grad, gate, kv_local, key_segments, got, other,
+        table, q, grad, tiles, kv_local, got, other,
         local_out, local_lse, out, lse, dscore,
     )
     swapped = lax.ppermute(given, "c", SWAP)

time: 118 us -> 117 us (level)
  other arithmetic: 6.56 us -> 3.22 us
  waiting for transfers between devices: 7.42 us -> 10 us
  Pallas kernels: 19.4 us -> 17.5 us
  blocking collectives: 13.7 us -> 15.5 us
    convert_element_type x2 -> x0, other arithmetic: 2.62 us -> none  [the longest x1 1.47 us: body(): key_segments = (segments[:, None] == lanes[None, :]).astype(jnp.bfloat16)]
    ppermute x1, starting transfers between devices: 6.71 us -> 4.67 us  [body(): back_back = lax.ppermute(parcel(back_slot), RUN, run_pairs(BACKWARD_BACK))]
    ppermute x1, starting transfers between devices: 7.29 us -> 9.33 us  [body(): lax.ppermute(parcel(far_slot), RUN, run_pairs(BACKWARD_FAR + BACKWARD_NEXT))]
    pallas_call x1, Pallas kernels: 5.29 us -> 3.32 us  [body(): pl.pallas_call(prompt_step, out_shape=(pltpu.VMEM((2 * PMAX, head_dim), j...]
    all_to_all x1, blocking collectives: 13.7 us -> 15.5 us  [body(): lax.all_to_all(spread, ('y', 'x'), split_axis=0, concat_axis=0, tiled=True)]
    ppermute x1, waiting for transfers between devices: 2.18 us -> 3.64 us  [body(): lax.ppermute(prompt_of(2 * h + c & NH - 1), RUN, run_pairs(FORWARD_BACK))]
  transfers between devices with their start and end apart: 9 -> 9, of which waited for: 4 -> 4; matrix products, arithmetic and copies ran while one was open for 7% -> 4% of each run, Pallas kernels for 12% -> 12%
where the time goes in v5:
time: 117 us
  starting transfers between devices  61.4 us (52%)
  Pallas kernels  17.5 us (15%)
  blocking collectives  15.5 us (13%)
  waiting for transfers between devices  10 us (9%)
  local copies, waits for them, and re-layouts  6.91 us (6%)
  other arithmetic  3.22 us (3%)
  between operations  2.11 us (2%)
    ppermute x1, starting transfers between devices, body(): lax.ppermute(prompt_of(jnp.where(far_sender, head_far, head_next)), RUN,...  26.6 us
    all_to_all x1, blocking collectives, body(): lax.all_to_all(spread, ('y', 'x'), split_axis=0, concat_axis=0, tiled=True)  15.5 us
    ppermute x1, starting transfers between devices, body(): lax.ppermute(parcel(far_slot), RUN, run_pairs(BACKWARD_FAR + BACKWARD_NEXT))  9.33 us
    pallas_call x1, Pallas kernels, body(): pl.pallas_call(local_backward, out_shape=(narrow, narrow, part_shape, par...  7.56 us
    all_to_all x1, starting transfers between devices, body(): lax.all_to_all(outgoing, ('y', 'x'), split_axis=0, concat_axis=0, tiled=T...  6.75 us
    ppermute x1, starting transfers between devices, body(): lax.ppermute(prompt_of(2 * h + c & NH - 1), RUN, run_pairs(FORWARD_BACK))  5.17 us
    pallas_call x1, Pallas kernels, body(): pl.pallas_call(local_forward, out_shape=(wide, wide), name='local_forward...  4.79 us
    ppermute x1, starting transfers between devices, body(): back_back = lax.ppermute(parcel(back_slot), RUN, run_pairs(BACKWARD_BACK))  4.67 us
  transfers between devices with their start and end apart: 9, of which 4 were waited for; matrix products, arithmetic and copies ran while one was open for 4% of the time, Pallas kernels for 12%

profile of v5, /device:TPU:1, one launch (start us, length us, event | category | flops | bytes accessed | tf_op | source)
XLA Modules:
  0.0 116.7 jit_solution(15907603773788910112)
XLA Ops:
  0.7 1.4 %constant_dynamic-slice_fusion.4 = (bf16[64,2,1,128]{3,2,1,0:T(2,128)(2,1)S(1)}, bf16[64,2,1,128]{3,2,1,0:T(2,128)(2,1)S(1)}, bf16[64,2,1,128]{3,2,1,0:T(2,128)(2,1)S(1)}) fusion(bf16[512,2,8,128]{3,2,1,0:T(8,128)(2,1)} %param.7, u32[]{:T(128)S(6)} %convert_element_type.43, u32[]{:T(128)S(6)} %convert_element_type.44, u32[]{:T(128)S(6)} %convert_element_type.45), kind=kLoop, calls=%fused_computation.20 | loop fusion | bytes 196620 | tf_op jit(solution)/shard_map/dynamic_slice | solution.py:312
  2.1 26.6 %collective-permute-start.1 = (bf16[128,128]{1,0:T(8,128)(2,1)S(1)}, bf16[128,128]{1,0:T(8,128)(2,1)S(1)}, u32[]{:S(2)}, u32[]{:S(2)}) collective-permute-start(bf16[128,128]{1,0:T(8,128)(2,1)S(1)} %bitcast.51), channel_id=1, source_target_pairs={{12,128},{13,130},{14,132},{15,134},{0,136},{1,138},{2,140},{3,142... | collective-permute-start | bytes 98312 | tf_op jit(solution)/shard_map/ppermute | solution.py:320
  28.7 5.2 %collective-permute-start = (bf16[128,128]{1,0:T(8,128)(2,1)S(1)}, bf16[128,128]{1,0:T(8,128)(2,1)S(1)}, u32[]{:S(2)}, u32[]{:S(2)}) collective-permute-start(bf16[128,128]{1,0:T(8,128)(2,1)S(1)} %bitcast.52), channel_id=1, source_target_pairs={{0,193},{1,195},{2,197},{3,199},{4,201},{5,203},{6,205},{7,207},{6... | collective-permute-start | bytes 98312 | tf_op jit(solution)/shard_map/ppermute | solution.py:324
  33.9 2.1 %constant_dynamic-slice_fusion.1 = bf16[512,2,1,128]{3,2,1,0:T(2,128)(2,1)S(1)} fusion(bf16[512,2,8,128]{3,2,1,0:T(8,128)(2,1)} %param.7, u32[]{:T(128)S(6)} %convert_element_type.43), kind=kLoop, calls=%fused_computation.17 | loop fusion | bytes 524292 | tf_op jit(solution)/shard_map/jit(dynamic_index_in_dim)/dynamic_slice | solution.py:336
  36.0 1.9 %route.1 = (s32[16]{0:T(128)}, u32[1]{0:T(128)}, u32[1]{0:T(128)}, u32[1]{0:T(128)}, u32[1]{0:T(128)}, /*index=5*/u32[1]{0:T(128)}, u32[1]{0:T(128)}) custom-call(s32[64]{0:T(128)} %partner_ref.1, s32[64]{0:T(128)} %blocks_ref.1, s32[4,128]{1,0:T(4,128)} %bitcast.53), custom_call_target="tpu_custom_call" | custom-call | tf_op jit(solution)/shard_map/route/pallas_call | solution.py:330
  38.6 0.8 copy.18
  39.4 3.6 %collective-permute-done = bf16[128,128]{1,0:T(8,128)(2,1)S(1)} collective-permute-done((bf16[128,128]{1,0:T(8,128)(2,1)S(1)}, bf16[128,128]{1,0:T(8,128)(2,1)S(1)}, u32[]{:S(2)}, u32[]{:S(2)}) %collective-permute-start) | collective-permute-done | bytes 32800 | tf_op jit(solution)/shard_map/ppermute | solution.py:324
  43.0 0.9 broadcast_select_fusion.1
  43.9 6.8 %all-to-all-start = ((bf16[16,128,128]{2,1,0:T(8,128)(2,1)}), bf16[16,128,128]{2,1,0:T(8,128)(2,1)S(1)}, u32[]{:S(2)}, u32[]{:S(2)}) async-start(bf16[16,128,128]{2,1,0:T(8,128)(2,1)} %broadcast_select_fusion.1), calls=%async_computation | async-start | bytes 1048576 | tf_op jit(solution)/shard_map/all_to_all | solution.py:351
  50.7 4.8 %local_forward.1 = (f32[2048,128]{1,0:T(8,128)}, f32[2048,128]{1,0:T(8,128)}) custom-call(bf16[2048,128]{1,0:T(8,128)(2,1)} %bitcast.44, s32[4,128]{1,0:T(4,128)} %bitcast.54, bf16[2,512,128]{2,1,0:T(8,128)(2,1)} %bitcast.47), custom_call_target="tpu_custom_call" | custom-call | tf_op jit(solution)/shard_map/local_forward/pallas_call | solution.py:352
  55.5 4.2 %all-to-all-done = bf16[16,128,128]{2,1,0:T(8,128)(2,1)S(1)} async-done(((bf16[16,128,128]{2,1,0:T(8,128)(2,1)}), bf16[16,128,128]{2,1,0:T(8,128)(2,1)S(1)}, u32[]{:S(2)}, u32[]{:S(2)}) %all-to-all-start) | async-done | bytes 524320 | tf_op jit(solution)/shard_map/all_to_all | solution.py:351
  60.3 1.9 %collective-permute-start.2 = (bf16[128,128]{1,0:T(8,128)(2,1)S(1)}, bf16[128,128]{1,0:T(8,128)(2,1)S(1)}, u32[]{:S(2)}, u32[]{:S(2)}) collective-permute-start(bf16[128,128]{1,0:T(8,128)(2,1)S(1)} %dynamic-slice_bitcast_fusion.2.got_ref), channel_id=1, source_target_pairs={{0,1},{1,0},{2,3},{3,2},{4,5},{5,4},{6,7},{7,6},{8,9},{9,8},{10,11... | collective-permute-start | bytes 98312 | tf_op jit(solution)/shard_map/ppermute | solution.py:358
  62.3 1.2 %collective-permute-done.2.other_ref = bf16[128,128]{1,0:T(8,128)(2,1)S(1)} collective-permute-done((bf16[128,128]{1,0:T(8,128)(2,1)S(1)}, bf16[128,128]{1,0:T(8,128)(2,1)S(1)}, u32[]{:S(2)}, u32[]{:S(2)}) %collective-permute-start.2) | collective-permute-done | bytes 32800 | tf_op jit(solution)/shard_map/ppermute | solution.py:358
  63.4 3.3 %prompt_step.1 = (bf16[128,128]{1,0:T(8,128)(2,1)S(1)}, f32[2048,128]{1,0:T(8,128)}, f32[2048,128]{1,0:T(8,128)}, bf16[2048,128]{1,0:T(8,128)(2,1)}) custom-call(s32[16]{0:T(128)} %get-tuple-element.25.scalars_ref, bf16[128,128]{1,0:T(8,128)(2,1)S(1)} %dynamic-slice_bitcast_fusion.2.got_ref, bf16[128,128]{1,0:T(8,128)(2,1)S(1)} %collective-permute-done.2.other_ref, ...), custom_call_target="tpu_custom_call" | custom-call | tf_op jit(solution)/shard_map/prompt_step/pallas_call | solution.py:360
  66.8 2.1 %collective-permute-start.4 = (bf16[128,128]{1,0:T(8,128)(2,1)S(1)}, bf16[128,128]{1,0:T(8,128)(2,1)S(1)}, u32[]{:S(2)}, u32[]{:S(2)}) collective-permute-start(bf16[128,128]{1,0:T(8,128)(2,1)S(1)} %get-tuple-element.43), channel_id=1, source_target_pairs={{0,1},{1,0},{2,3},{3,2},{4,5},{5,4},{6,7},{7,6},{8,9},{9,8},{10,11... | collective-permute-start | bytes 98312 | tf_op jit(solution)/shard_map/ppermute | solution.py:378
  68.9 1.0 collective-permute-done.4
  70.0 15.5 %all_to_all.10 = bf16[16,128,128]{2,1,0:T(8,128)(2,1)S(1)} all-to-all(bf16[16,128,128]{2,1,0:T(8,128)(2,1)S(1)} %broadcast_select_fusion), channel_id=1, replica_groups=mesh['y'=4,'w'=4,'x'=4,'h'=8,'c'=2] {'y','x'}, dimensions={0} | all-to-all | bytes 1048576 | tf_op jit(solution)/shard_map/all_to_all | solution.py:383
  85.5 1.3 %dynamic-slice_bitcast_fusion = (bf16[128,128]{1,0:T(8,128)(2,1)S(1)}, bf16[128,128]{1,0:T(8,128)(2,1)S(1)}) fusion(bf16[16,128,128]{2,1,0:T(8,128)(2,1)S(1)} %all_to_all.10, u32[]{:T(128)} %bitcast.25, u32[]{:T(128)} %bitcast.21), kind=kLoop, calls=%fused_computation.12 | loop fusion | bytes 131080 | tf_op jit(solution)/shard_map/jit(dynamic_index_in_dim)/squeeze | solution.py:386
  86.8 9.3 %collective-permute-start.5 = (bf16[128,128]{1,0:T(8,128)(2,1)S(1)}, bf16[128,128]{1,0:T(8,128)(2,1)S(1)}, u32[]{:S(2)}, u32[]{:S(2)}) collective-permute-start(bf16[128,128]{1,0:T(8,128)(2,1)S(1)} %get-tuple-element.51), channel_id=1, source_target_pairs={{0,128},{2,130},{4,132},{6,134},{8,136},{10,138},{12,140},{14,142}... | collective-permute-start | bytes 98312 | tf_op jit(solution)/shard_map/ppermute | solution.py:388
  96.2 4.7 %collective-permute-start.6 = (bf16[128,128]{1,0:T(8,128)(2,1)S(1)}, bf16[128,128]{1,0:T(8,128)(2,1)S(1)}, u32[]{:S(2)}, u32[]{:S(2)}) collective-permute-start(bf16[128,128]{1,0:T(8,128)(2,1)S(1)} %get-tuple-element.50), channel_id=1, source_target_pairs={{1,193},{3,195},{5,197},{7,199},{9,201},{11,203},{13,205},{15,207}... | collective-permute-start | bytes 98312 | tf_op jit(solution)/shard_map/ppermute | solution.py:391
  102.0 7.6 %local_backward.1 = (bf16[2048,128]{1,0:T(8,128)(2,1)}, bf16[2048,128]{1,0:T(8,128)(2,1)}, bf16[512,128]{1,0:T(8,128)(2,1)}, bf16[512,128]{1,0:T(8,128)(2,1)}) custom-call(s32[16]{0:T(128)} %get-tuple-element.25.scalars_ref, bf16[2048,128]{1,0:T(8,128)(2,1)} %bitcast.46, bf16[2048,128]{1,0:T(8,128)(2,1)} %bitcast.50, s32[4,128]{1,0:T(4,128)} %bitcast.55, ...), custom_call_target="tpu_custom_call" | custom-call | tf_op jit(solution)/shard_map/local_backward/pallas_call | solution.py:394
  109.6 1.9 %collective-permute-start.3 = (bf16[512,128]{1,0:T(8,128)(2,1)}, bf16[512,128]{1,0:T(8,128)(2,1)S(1)}, u32[]{:S(2)}, u32[]{:S(2)}) collective-permute-start(bf16[512,128]{1,0:T(8,128)(2,1)} %get-tuple-element.41), channel_id=1, source_target_pairs={{0,1},{1,0},{2,3},{3,2},{4,5},{5,4},{6,7},{7,6},{8,9},{9,8},{10,11... | collective-permute-start | bytes 393224 | tf_op jit(solution)/shard_map/ppermute | solution.py:405
  112.1 2.9 %collective-permute-start.7 = (bf16[64,128]{1,0:T(8,128)(2,1)S(1)}, bf16[64,128]{1,0:T(8,128)(2,1)S(1)}, u32[]{:S(2)}, u32[]{:S(2)}) collective-permute-start(bf16[64,128]{1,0:T(8,128)(2,1)S(1)} %constant_dynamic-slice_fusion), channel_id=1, source_target_pairs={{0,1},{1,0},{2,3},{3,2},{4,5},{5,4},{6,7},{7,6},{8,9},{9,8},{10,11... | collective-permute-start | bytes 49160 | tf_op jit(solution)/shard_map/ppermute | solution.py:414
  115.1 0.9 convert_add_fusion
  (23 shorter events, 2.7 us)
Async XLA Ops:
  2.1 41.0 %collective-permute-start.1 = (bf16[128,128]{1,0:T(8,128)(2,1)S(1)}, bf16[128,128]{1,0:T(8,128)(2,1)S(1)}, u32[]{:S(2)}, u32[]{:S(2)}) collective-permute-start(bf16[128,128]{1,0:T(8,128)(2,1)S(1)} %bitcast.51), channel_id=1, source_target_pairs={{12,128},{13,130},{14,132},{15,134},{0,136},{1,138},{2,140},{3,142... | collective-permute-start | bytes 98312 | tf_op jit(solution)/shard_map/ppermute | solution.py:320
  28.7 14.3 %collective-permute-start = (bf16[128,128]{1,0:T(8,128)(2,1)S(1)}, bf16[128,128]{1,0:T(8,128)(2,1)S(1)}, u32[]{:S(2)}, u32[]{:S(2)}) collective-permute-start(bf16[128,128]{1,0:T(8,128)(2,1)S(1)} %bitcast.52), channel_id=1, source_target_pairs={{0,193},{1,195},{2,197},{3,199},{4,201},{5,203},{6,205},{7,207},{6... | collective-permute-start | bytes 98312 | tf_op jit(solution)/shard_map/ppermute | solution.py:324
  43.9 15.8 %all-to-all-start = ((bf16[16,128,128]{2,1,0:T(8,128)(2,1)}), bf16[16,128,128]{2,1,0:T(8,128)(2,1)S(1)}, u32[]{:S(2)}, u32[]{:S(2)}) async-start(bf16[16,128,128]{2,1,0:T(8,128)(2,1)} %broadcast_select_fusion.1), calls=%async_computation | async-start | bytes 1048576 | tf_op jit(solution)/shard_map/all_to_all | solution.py:351
  60.3 25.2 %copy-start = (bf16[128,128]{1,0:T(8,128)(2,1)}, bf16[128,128]{1,0:T(8,128)(2,1)S(1)}, u32[]{:S(2)}) copy-start(bf16[128,128]{1,0:T(8,128)(2,1)S(1)} %dynamic-slice_bitcast_fusion.2.got_ref) | copy-start | bytes 98308
  60.3 3.1 %collective-permute-start.2 = (bf16[128,128]{1,0:T(8,128)(2,1)S(1)}, bf16[128,128]{1,0:T(8,128)(2,1)S(1)}, u32[]{:S(2)}, u32[]{:S(2)}) collective-permute-start(bf16[128,128]{1,0:T(8,128)(2,1)S(1)} %dynamic-slice_bitcast_fusion.2.got_ref), channel_id=1, source_target_pairs={{0,1},{1,0},{2,3},{3,2},{4,5},{5,4},{6,7},{7,6},{8,9},{9,8},{10,11... | collective-permute-start | bytes 98312 | tf_op jit(solution)/shard_map/ppermute | solution.py:358
  63.4 22.1 %copy-start.1 = (bf16[128,128]{1,0:T(8,128)(2,1)}, bf16[128,128]{1,0:T(8,128)(2,1)S(1)}, u32[]{:S(2)}) copy-start(bf16[128,128]{1,0:T(8,128)(2,1)S(1)} %collective-permute-done.2.other_ref) | copy-start | bytes 98308
  66.8 3.1 %collective-permute-start.4 = (bf16[128,128]{1,0:T(8,128)(2,1)S(1)}, bf16[128,128]{1,0:T(8,128)(2,1)S(1)}, u32[]{:S(2)}, u32[]{:S(2)}) collective-permute-start(bf16[128,128]{1,0:T(8,128)(2,1)S(1)} %get-tuple-element.43), channel_id=1, source_target_pairs={{0,1},{1,0},{2,3},{3,2},{4,5},{5,4},{6,7},{7,6},{8,9},{9,8},{10,11... | collective-permute-start | bytes 98312 | tf_op jit(solution)/shard_map/ppermute | solution.py:378
  86.8 24.7 %collective-permute-start.5 = (bf16[128,128]{1,0:T(8,128)(2,1)S(1)}, bf16[128,128]{1,0:T(8,128)(2,1)S(1)}, u32[]{:S(2)}, u32[]{:S(2)}) collective-permute-start(bf16[128,128]{1,0:T(8,128)(2,1)S(1)} %get-tuple-element.51), channel_id=1, source_target_pairs={{0,128},{2,130},{4,132},{6,134},{8,136},{10,138},{12,140},{14,142}... | collective-permute-start | bytes 98312 | tf_op jit(solution)/shard_map/ppermute | solution.py:388
  96.2 15.4 %collective-permute-start.6 = (bf16[128,128]{1,0:T(8,128)(2,1)S(1)}, bf16[128,128]{1,0:T(8,128)(2,1)S(1)}, u32[]{:S(2)}, u32[]{:S(2)}) collective-permute-start(bf16[128,128]{1,0:T(8,128)(2,1)S(1)} %get-tuple-element.50), channel_id=1, source_target_pairs={{1,193},{3,195},{5,197},{7,199},{9,201},{11,203},{13,205},{15,207}... | collective-permute-start | bytes 98312 | tf_op jit(solution)/shard_map/ppermute | solution.py:391
  109.6 5.5 %collective-permute-start.3 = (bf16[512,128]{1,0:T(8,128)(2,1)}, bf16[512,128]{1,0:T(8,128)(2,1)S(1)}, u32[]{:S(2)}, u32[]{:S(2)}) collective-permute-start(bf16[512,128]{1,0:T(8,128)(2,1)} %get-tuple-element.41), channel_id=1, source_target_pairs={{0,1},{1,0},{2,3},{3,2},{4,5},{5,4},{6,7},{7,6},{8,9},{9,8},{10,11... | collective-permute-start | bytes 393224 | tf_op jit(solution)/shard_map/ppermute | solution.py:405
  112.1 3.9 %collective-permute-start.7 = (bf16[64,128]{1,0:T(8,128)(2,1)S(1)}, bf16[64,128]{1,0:T(8,128)(2,1)S(1)}, u32[]{:S(2)}, u32[]{:S(2)}) collective-permute-start(bf16[64,128]{1,0:T(8,128)(2,1)S(1)} %constant_dynamic-slice_fusion), channel_id=1, source_target_pairs={{0,1},{1,0},{2,3},{3,2},{4,5},{5,4},{6,7},{7,6},{8,9},{9,8},{10,11... | collective-permute-start | bytes 49160 | tf_op jit(solution)/shard_map/ppermute | solution.py:414
  116.1 0.7 copy-start.2
